TPU v7x, 32 devices: a whole 2x2x4 slice. The times are simulated.
32 devices in a mesh: groups: 1, seq: 32 (over z, y, x, core).
Axes of the slice: x: 2, y: 2, z: 4, core: 2. Of those that a mesh axis runs over, the one named last changes fastest.
Arguments:
- queries: bfloat16 [8192, 2048], P(('groups', 'seq')), may hold values from -6 to 6
- keys: bfloat16 [8192, 2048], P(('groups', 'seq')), may hold values from -6 to 6
- values: bfloat16 [8192, 2048], P(('groups', 'seq')), may hold values from -6 to 6
- out_weight: bfloat16 [2048, 2048], replicated, may hold values from -0.125 to 0.125
- out_grad: bfloat16 [8192, 2048], P(('groups', 'seq')), may hold values from -6 to 6
Outputs:
- query_grad: bfloat16 [8192, 2048], P(('groups', 'seq'))
- key_grad: bfloat16 [8192, 2048], P(('groups', 'seq'))
- value_grad: bfloat16 [8192, 2048], P(('groups', 'seq'))
- weight_grad: float32 [2048, 2048], P(('groups', 'seq'))
All inputs are finite; a program needn't handle non-finite values.
Results may differ from a plain program's by a relative error of at most 0.0033.
Values sent between devices are 32-bit elements; how exact they have to be, the bound alone decides.
A program may use at most 192 MiB of HBM per device.

v0:
```python
import jax
import jax.numpy as jnp
from jax import lax
from jax.sharding import PartitionSpec as P

HEADS = 16
HEAD = 128


def entering(part, axis, combine, identity, reverse):
    count = lax.axis_size(axis)
    place = lax.axis_index(axis)
    ahead = count - 1 - place if reverse else place
    gathered = jax.tree.map(lambda a: lax.all_gather(a, axis), part)
    state = jax.tree.map(lambda a, e: jnp.zeros_like(a) + jnp.asarray(e, a.dtype), part, identity)

    def one(turn, state):
        source = count - 1 - turn if reverse else turn
        return combine(
            state, jax.tree.map(lambda a: lax.dynamic_index_in_dim(a, source, 0, False), gathered)
        )

    return lax.fori_loop(0, ahead, one, state)


def feature(x):
    return jax.nn.elu(x) + 1.0


def attend_block(query_f, key_f, value_f, state, zsum):
    block_len = query_f.shape[0]
    fq = feature(query_f.reshape(block_len, HEADS, HEAD))
    fk = feature(key_f.reshape(block_len, HEADS, HEAD))
    vv = value_f.reshape(block_len, HEADS, HEAD)
    rows = lax.broadcasted_iota(jnp.int32, (block_len, block_len), 0)
    cols = lax.broadcasted_iota(jnp.int32, (block_len, block_len), 1)
    causal = (cols <= rows).astype(jnp.float32)
    scores = jnp.einsum("thd,shd->hts", fq, fk, precision=lax.Precision.HIGHEST) * causal[None]
    numer = jnp.einsum("hts,she->the", scores, vv, precision=lax.Precision.HIGHEST)
    numer = numer + jnp.einsum("thd,hde->the", fq, state, precision=lax.Precision.HIGHEST)
    denom = jnp.sum(scores, axis=2).T + jnp.einsum(
        "thd,hd->th", fq, zsum, precision=lax.Precision.HIGHEST
    )
    return (numer / denom[:, :, None]).reshape(block_len, HEADS * HEAD)


def summarize(key_f, value_f):
    block_len = key_f.shape[0]
    fk = feature(key_f.reshape(block_len, HEADS, HEAD))
    vv = value_f.reshape(block_len, HEADS, HEAD)
    state = jnp.einsum("thd,the->hde", fk, vv, precision=lax.Precision.HIGHEST)
    return (state, jnp.sum(fk, axis=0))


def add_pair(earlier, later):
    return (earlier[0] + later[0], earlier[1] + later[1])


def body(queries, keys, values, out_weight, out_grad):
    query_f = queries.astype(jnp.float32)
    key_f = keys.astype(jnp.float32)
    value_f = values.astype(jnp.float32)
    zeros_pair = (
        jnp.zeros((HEADS, HEAD, HEAD), jnp.float32),
        jnp.zeros((HEADS, HEAD), jnp.float32),
    )
    local_state, pull_state = jax.vjp(summarize, key_f, value_f)
    state_in, zsum_in = entering(local_state, "seq", add_pair, zeros_pair, False)
    attended, pull_attend = jax.vjp(attend_block, query_f, key_f, value_f, state_in, zsum_in)
    rounded = attended.astype(jnp.bfloat16)
    attended_grad = lax.dot_general(
        out_grad, out_weight, (((1,), (1,)), ((), ())), preferred_element_type=jnp.float32
    )
    query_part, key_part, value_part, state_grad, zsum_grad = pull_attend(attended_grad)
    later_state = entering((state_grad, zsum_grad), "seq", add_pair, zeros_pair, True)
    key_extra, value_extra = pull_state(later_state)
    weight_grad = lax.psum_scatter(
        lax.dot_general(
            rounded, out_grad, (((0,), (0,)), ((), ())), preferred_element_type=jnp.float32
        ),
        "seq",
        scatter_dimension=0,
        tiled=True,
    )
    query_grad = query_part.astype(jnp.bfloat16)
    key_grad = (key_part + key_extra).astype(jnp.bfloat16)
    value_grad = (value_part + value_extra).astype(jnp.bfloat16)
    return (query_grad, key_grad, value_grad, weight_grad)


def solution(mesh):
    placed = (
        P(("groups", "seq"), None),
        P(("groups", "seq"), None),
        P(("groups", "seq"), None),
        P(),
        P(("groups", "seq"), None),
    )
    return jax.shard_map(
        body,
        mesh=mesh,
        in_specs=placed,
        out_specs=(
            P(("groups", "seq"), None),
            P(("groups", "seq"), None),
            P(("groups", "seq"), None),
            P(("groups", "seq"), None),
        ),
        check_vma=False,
    )
```

profile of v0, /device:TPU:0, one launch (start us, length us, event | category | flops | bytes accessed | tf_op | source)
XLA Modules:
  0.0 676.5 jit_solution(14905975301412319601)
XLA Ops:
  7.2 1.6 copy.33
  8.8 4.9 fusion.43
  13.8 2.6 copy.32
  16.3 2.2 fusion.8
  18.5 48.0 %all_gather.27 = f32[32,16,128]{2,1,0:T(8,128)} all-gather(f32[1,16,128]{2,1,0:T(8,128)S(1)} %bitcast.170), channel_id=1, replica_groups=mesh['groups'=1,'seq'=32] {'seq'}, dimensions={0}, use_global_device_ids=true | all-gather | bytes 270336 | tf_op jit(solution)/shard_map/all_gather | solution.py:14
  66.6 9.4 %multiply_reduce_fusion = (f32[16,256]{1,0:T(8,128)S(1)}, f32[16,256,256]{1,2,0:T(8,128)}) fusion(f32[256,256]{0,1:T(8,128)S(1)} %fusion.49, f32[256,16,128]{0,2,1:T(8,128)S(1)} %bitcast.151, f32[256,16,128]{0,2,1:T(8,128)} %bitcast.155), kind=kOutput, calls=%fused_computation.13 | convolution fusion | flops 1616900096 | bytes 8667136 | tf_op jit(solution)/shard_map/jvp(thd,shd->hts)/dot_general | solution.py:38
  76.0 7.2 %fusion.67 = f32[256,2048]{0,1:T(8,128)} fusion(bf16[256,2048]{1,0:T(8,128)(2,1)S(1)} %copy-done, bf16[2048,2048]{1,0:T(8,128)(2,1)} %param.12), kind=kOutput, calls=%fused_computation.80 | convolution fusion | flops 2147483648 | bytes 11534336 | tf_op jit(solution)/shard_map/transpose(jvp())/reshape | solution.py:44
  83.2 129.2 %all-gather.6.cloned.1.call-done = f32[512,128,128]{2,1,0:T(8,128)} async-done(((f32[16,128,128]{2,1,0:T(8,128)}), f32[512,128,128]{2,1,0:T(8,128)}) %all-gather.6.cloned.1.call-update) | async-done | bytes 33554448 | tf_op jit(solution)/shard_map/all_gather | solution.py:14
  213.0 3.6 fusion.63
  216.6 5.5 fusion.24
  222.2 4.5 fusion.61
  226.7 4.3 divide_convert_fusion
  231.0 8.1 %fusion.68 = f32[2048,2048]{1,0:T(8,128)} fusion(bf16[256,2048]{0,1:T(8,128)(2,1)S(1)} %bitcast.163, bf16[256,2048]{1,0:T(8,128)(2,1)S(1)} %copy-done), kind=kOutput, calls=%fused_computation.81 | convolution fusion | flops 2147483648 | bytes 18874368 | tf_op jit(solution)/shard_map/dot_general | solution.py:78
  240.3 3.8 fusion.26
  244.2 4.1 fusion.1
  248.2 3.1 fusion.19
  253.3 2.5 fusion.51
  255.8 107.7 %all-gather.2 = f32[512,128]{1,0:T(8,128)S(1)} all-gather(f32[16,128]{1,0:T(8,128)S(1)} %bitcast.171), channel_id=4, replica_groups=mesh['groups'=1,'seq'=32] {'seq'}, dimensions={0}, use_global_device_ids=true | all-gather | bytes 270336 | tf_op jit(solution)/shard_map/all_gather | solution.py:14
  363.4 9.3 %fusion = f32[16,256,128]{1,2,0:T(8,128)} fusion(f32[16,256,256]{1,2,0:T(8,128)} %copy-done.7, f32[16,256]{1,0:T(8,128)S(1)} %get-tuple-element.160, f32[256,256]{0,1:T(8,128)S(1)} %fusion.49, f32[256,16,128]{0,2,1:T(8,128)S(1)} %bitcast.161), kind=kOutput, calls=%fused_computation.7 | convolution fusion | flops 1614807040 | bytes 8667136 | tf_op jit(solution)/shard_map/transpose(jvp(thd,shd->hts))/dot_general | solution.py:38
  372.8 5.8 fusion.2
  378.6 107.3 %all-gather.8.cloned.1.call-done = f32[512,128,128]{2,1,0:T(8,128)} async-done(((f32[16,128,128]{2,1,0:T(8,128)}), f32[512,128,128]{2,1,0:T(8,128)}) %all-gather.8.cloned.1.call-update) | async-done | bytes 33554448 | tf_op jit(solution)/shard_map/all_gather | solution.py:14
  486.0 48.1 %while.27 = (s32[]{:T(128)}, f32[16,128,128]{2,1,0:T(8,128)S(1)}, f32[16,128]{1,0:T(8,128)S(1)}, s32[]{:T(128)}, f32[32,16,128,128]{3,2,1,0:T(8,128)}, /*index=5...) while((s32[]{:T(128)}, f32[16,128,128]{2,1,0:T(8,128)S(1)}, ...), condition=%wide.region_6.7_spmd, body=%wide.region_5.6_spmd.sunk | while | flops 264198 | bytes 3170467 | solution.py:23
  486.1 1.5 bitcast_add_fusion.12
  487.6 1.5 bitcast_add_fusion.12
  489.1 1.5 bitcast_add_fusion.12
  490.7 1.5 bitcast_add_fusion.12
  492.2 1.7 bitcast_add_fusion.12
  493.9 1.5 bitcast_add_fusion.12
  495.4 1.5 bitcast_add_fusion.12
  500.0 1.5 bitcast_add_fusion.12
  501.6 1.5 bitcast_add_fusion.12
  503.1 1.5 bitcast_add_fusion.12
  504.7 1.5 bitcast_add_fusion.12
  510.8 1.5 bitcast_add_fusion.12
  512.4 1.5 bitcast_add_fusion.12
  513.9 1.5 bitcast_add_fusion.12
  515.5 1.5 bitcast_add_fusion.12
  520.1 1.5 bitcast_add_fusion.12
  521.6 1.5 bitcast_add_fusion.12
  523.2 1.5 bitcast_add_fusion.12
  524.7 1.5 bitcast_add_fusion.12
  526.3 1.5 bitcast_add_fusion.12
  527.8 1.5 bitcast_add_fusion.12
  529.4 1.5 bitcast_add_fusion.12
  530.9 1.5 bitcast_add_fusion.12
  534.2 5.0 add_convert_fusion
  540.6 5.1 fusion.11
  547.2 122.6 %reduce-scatter.2.cloned.1.call-done = f32[64,2048]{1,0:T(8,128)} async-done(((f32[2048,2048]{1,0:T(8,128)}), f32[64,2048]{1,0:T(8,128)}) %reduce-scatter.2.cloned.1.call-update) | async-done | bytes 524304 | tf_op jit(solution)/shard_map/reduce_scatter | solution.py:77
  (84 shorter events, 19.1 us)
Async XLA Ops:
  7.2 68.8 %copy-start = (bf16[256,2048]{1,0:T(8,128)(2,1)S(1)}, bf16[256,2048]{1,0:T(8,128)(2,1)}, u32[]{:S(2)}) copy-start(bf16[256,2048]{1,0:T(8,128)(2,1)} %param.13) | copy-start | bytes 3145732
  7.2 205.2 %all-gather.6.cloned.1.call-start = ((), (), s32[]{:S(2)}) async-start(), calls=%async_computation.2 | async-start | bytes 34603008 | tf_op jit(solution)/shard_map/all_gather | solution.py:14
  8.8 57.8 %copy-start.2 = (f32[256,2048]{0,1:T(8,128)}, f32[256,2048]{0,1:T(8,128)S(1)}, u32[]{:S(2)}) copy-start(f32[256,2048]{0,1:T(8,128)S(1)} %copy.33) | copy-start | bytes 6291460
  13.7 472.2 %all-gather.8.cloned.1.call-start = ((), (), s32[]{:S(2)}) async-start(), calls=%async_computation.3 | async-start | bytes 34603008 | tf_op jit(solution)/shard_map/all_gather | solution.py:14
  212.9 3.7 copy-start.4
  222.1 447.7 %reduce-scatter.2.cloned.1.call-start = ((), (), s32[]{:S(2)}) async-start(), calls=%async_computation.1 | async-start | bytes 17301504 | tf_op jit(solution)/shard_map/reduce_scatter | solution.py:77
  222.2 4.5 copy-start.8
  222.2 4.5 copy-start.10
  239.1 1.2 copy-start.9
  240.3 3.8 copy-start.3
  244.1 4.1 copy-start.7
  244.1 4.1 copy-start.5
  244.1 4.1 copy-start.12
  251.4 2.0 copy-start.6
  363.4 9.3 %copy-start.11 = (f32[16,256,256]{1,2,0:T(8,128)S(1)}, f32[16,256,256]{1,2,0:T(8,128)}, u32[]{:S(2)}) copy-start(f32[16,256,256]{1,2,0:T(8,128)} %get-tuple-element.162) | copy-start | bytes 12582916
  363.4 9.3 %copy-start.13 = (f32[256,2048]{0,1:T(8,128)S(1)}, f32[256,2048]{0,1:T(8,128)}, u32[]{:S(2)}) copy-start(f32[256,2048]{0,1:T(8,128)} %fusion.67) | copy-start | bytes 6291460
  540.6 129.2 %copy-start.1 = (bf16[256,2048]{1,0:T(8,128)(2,1)S(1)}, bf16[256,2048]{1,0:T(8,128)(2,1)}, u32[]{:S(2)}) copy-start(bf16[256,2048]{1,0:T(8,128)(2,1)} %param.13) | copy-start | bytes 3145732
Sparse Core Ops, SparseCore 0:
  13.8 198.4 all-gather.5
  222.2 263.6 all-gather.7
  488.8 180.9 reduce-scatter.1
where the time goes:
time: 687 us; the launch traced here: 677 us
  waiting for transfers between devices  359 us (52%)
  blocking collectives  156 us (23%)
  matrix products  86.2 us (13%)
  other arithmetic  49.2 us (7%)
  between operations  14.2 us (2%)
  local copies, waits for them, and re-layouts  10.4 us (2%)
    all_gather x2, waiting for transfers between devices, entering(): gathered = jax.tree.map(lambda a: lax.all_gather(a, axis), part)  237 us
    all_gather x2, blocking collectives, entering(): gathered = jax.tree.map(lambda a: lax.all_gather(a, axis), part)  156 us
    reduce_scatter x1, waiting for transfers between devices, body(): lax.psum_scatter(lax.dot_general(rounded, out_grad, (((0,), (0,)), ((), (...  123 us
    add x62, other arithmetic, add_pair(): return (earlier[0] + later[0], earlier[1] + later[1])  47 us
    dot_general x3, matrix products, attend_block(): jnp.einsum('thd,shd->hts', fq, fk, precision=lax.Precision.HIGHEST)  22.8 us
    dot_general x3, matrix products, summarize(): state = jnp.einsum('thd,the->hde', fk, vv, precision=lax.Precision.HIGHEST)  15 us
    dot_general x3, matrix products, attend_block(): jnp.einsum('hts,she->the', scores, vv, precision=lax.Precision.HIGHEST)  13.9 us
  transfers between devices with their start and end apart: 3, of which 3 were waited for; matrix products, arithmetic and copies ran while one was open for 19% of the time, Pallas kernels for 0%

commit v1 on v0

v1 whole, which is shorter than its diff:
```python
import functools

import jax
import jax.numpy as jnp
from jax import lax
from jax.experimental import pallas as pl
from jax.experimental.pallas import tpu as pltpu
from jax.sharding import PartitionSpec as P

HEAD = 128
MESH = pl.DeviceIdType.MESH
BF = jnp.bfloat16
F32 = jnp.float32
NN = (((1,), (0,)), ((), ()))
NT = (((1,), (1,)), ((), ()))
TN = (((0,), (0,)), ((), ()))


def split(x):
    if isinstance(x, tuple):
        return x
    if x.dtype == BF:
        return (x,)
    high = x.astype(BF)
    return (high, (x - high.astype(F32)).astype(BF))


def mm(a, b, dims):
    a, b = split(a), split(b)
    total = lax.dot_general(a[0], b[0], dims, preferred_element_type=F32)
    if len(a) > 1:
        total += lax.dot_general(a[1], b[0], dims, preferred_element_type=F32)
    if len(b) > 1:
        total += lax.dot_general(a[0], b[1], dims, preferred_element_type=F32)
    return total


def bits_of(n):
    count = n.bit_length() - 1
    assert 1 << count == n
    return count


def partner_of(me, k):
    return me + (1 - 2 * ((me // (1 << k)) % 2)) * (1 << k)


def scan_kernel(n, reverse, x_ref, e_ref, tot, recv, near, out, su, ru, sd, rd):
    me = lax.axis_index("seq")
    levels = bits_of(n)
    rows = x_ref.shape[0]
    barrier = pltpu.get_barrier_semaphore()
    for k in range(levels):
        pl.semaphore_signal(barrier, inc=1, device_id={"seq": partner_of(me, k)}, device_id_type=MESH)
    pl.semaphore_wait(barrier, levels)
    base = 0
    keeps = []
    for k in range(levels):
        half = rows >> (k + 1)
        off = rows - (rows >> k)
        bit = (me // (1 << k)) % 2
        keep = pl.multiple_of(base + bit * half, 8)
        give = pl.multiple_of(base + (1 - bit) * half, 8)
        src = x_ref if k == 0 else tot
        buf = recv.at[pl.ds(off, half)]
        copy = pltpu.make_async_remote_copy(
            src_ref=src.at[pl.ds(give, half)], dst_ref=buf, send_sem=su.at[k], recv_sem=ru.at[k],
            device_id={"seq": partner_of(me, k)}, device_id_type=MESH)
        copy.start()
        copy.wait()
        mine = src[pl.ds(keep, half), :]
        theirs = recv[pl.ds(off, half), :]
        first = jnp.where(bit == (1 if reverse else 0), mine, theirs)
        near[pl.ds(off, half), :] = first
        if k + 1 < levels:
            tot[pl.ds(keep, half), :] = mine + theirs
        keeps.append((keep, half, off, bit))
        base = keep
    e_ref[pl.ds(base, rows >> levels), :] = jnp.zeros((rows >> levels, x_ref.shape[1]), F32)
    for k in reversed(range(levels)):
        keep, half, off, bit = keeps[k]
        early = bit == (1 if reverse else 0)
        now = e_ref[pl.ds(keep, half), :]
        past = now + near[pl.ds(off, half), :]
        out[pl.ds(off, half), :] = jnp.where(early, past, now)
        copy = pltpu.make_async_remote_copy(
            src_ref=out.at[pl.ds(off, half)], dst_ref=e_ref.at[pl.ds(keep, half)],
            send_sem=sd.at[k], recv_sem=rd.at[k],
            device_id={"seq": partner_of(me, k)}, device_id_type=MESH)
        copy.start()
        e_ref[pl.ds(keep, half), :] = jnp.where(early, now, past)
        copy.wait()


def entering(x, n, reverse, collective_id):
    levels = bits_of(n)
    rows, cols = x.shape
    return pl.pallas_call(
        functools.partial(scan_kernel, n, reverse),
        out_shape=jax.ShapeDtypeStruct(x.shape, F32),
        in_specs=[pl.BlockSpec(memory_space=pltpu.VMEM)],
        out_specs=pl.BlockSpec(memory_space=pltpu.VMEM),
        scratch_shapes=[pltpu.VMEM((rows, cols), F32)] * 4 + [pltpu.SemaphoreType.DMA((levels,))] * 4,
        compiler_params=pltpu.CompilerParams(
            collective_id=collective_id, has_side_effects=True, vmem_limit_bytes=24 << 20),
        cost_estimate=pl.CostEstimate(flops=0, bytes_accessed=100_000_000, transcendentals=0),
    )(x)


def features(x):
    x = x.astype(F32)
    low = jnp.exp(jnp.minimum(x, 0.0))
    return jnp.where(x > 0, x + 1.0, low), low


def with_row(block, row, pad):
    row = jnp.where(lax.broadcasted_iota(jnp.int32, (pad - HEAD, HEAD), 0) == 0, row, 0.0)
    return jnp.concatenate([block, row], axis=0)


def sum_kernel(k_ref, v_ref, x_ref):
    fk, _ = features(k_ref[...])
    x_ref[...] = with_row(mm(v_ref[...], fk, TN), jnp.sum(fk, axis=0, keepdims=True), x_ref.shape[0])


def forward_of(q, k, v, entry):
    fq, qslope = features(q)
    fk, kslope = features(k)
    t = fq.shape[0]
    causal = lax.broadcasted_iota(jnp.int32, (t, t), 1) <= lax.broadcasted_iota(jnp.int32, (t, t), 0)
    fq_s, fk_s = split(fq), split(fk)
    scores = jnp.where(causal, mm(fq_s, fk_s, NT), 0.0)
    z = entry[HEAD:HEAD + 1, :]
    den = jnp.sum(scores, axis=1, keepdims=True) + jnp.sum(fq * z, axis=1, keepdims=True)
    scores = split(scores)
    numer = mm(scores, v, NN) + mm(fq_s, entry[:HEAD, :], NT)
    inv = 1.0 / den
    return fq, fq_s, qslope, fk_s, causal, scores, z, inv, numer * inv


def attend_kernel(q_ref, k_ref, v_ref, e_ref, da_ref, r_ref, g_ref):
    fq, fq_s, _, _, _, _, _, inv, att = forward_of(q_ref[...], k_ref[...], v_ref[...], e_ref[...])
    r_ref[...] = att.astype(BF)
    dn = da_ref[...] * inv
    dden = -jnp.sum(dn * att, axis=1, keepdims=True)
    g_ref[...] = with_row(mm(dn, fq_s, TN), jnp.sum(fq * dden, axis=0, keepdims=True), g_ref.shape[0])


def local_kernel(q_ref, k_ref, v_ref, e_ref, da_ref, dq_ref, dk_ref, dv_ref):
    v = v_ref[...]
    fq, fq_s, qslope, fk_s, causal, scores, z, inv, att = forward_of(q_ref[...], k_ref[...], v, e_ref[...])
    dn = da_ref[...] * inv
    dden = -jnp.sum(dn * att, axis=1, keepdims=True)
    dn_b = split(dn)
    dp = split(jnp.where(causal, mm(dn_b, v, NT) + dden, 0.0))
    dfq = mm(dp, fk_s, NN) + mm(dn_b, e_ref[:HEAD, :], NN) + dden * z
    dq_ref[...] = (dfq * qslope).astype(BF)
    dk_ref[...] = mm(dp, fq_s, TN)
    dv_ref[...] = mm(scores, dn_b, TN)


def finish_kernel(k_ref, v_ref, g_ref, dk_ref, dv_ref, ok_ref, ov_ref):
    fk, kslope = features(k_ref[...])
    g = split(g_ref[:HEAD, :])
    dfk = dk_ref[...] + mm(v_ref[...], g, NN) + g_ref[HEAD:HEAD + 1, :]
    ok_ref[...] = (dfk * kslope).astype(BF)
    ov_ref[...] = (dv_ref[...] + mm(fk, g, NT)).astype(BF)


def per_head(kernel, heads, tokens, pad, ins, outs, args):
    spec = {
        "t": pl.BlockSpec((tokens, HEAD), lambda h: (0, h)),
        "s": pl.BlockSpec((pad, HEAD), lambda h: (h, 0)),
    }
    shape = {"t": (tokens, heads * HEAD), "s": (heads * pad, HEAD)}
    return pl.pallas_call(
        kernel,
        grid=(heads,),
        in_specs=[spec[i] for i in ins],
        out_specs=[spec[o] for o, _ in outs],
        out_shape=[jax.ShapeDtypeStruct(shape[o], d) for o, d in outs],
        compiler_params=pltpu.CompilerParams(vmem_limit_bytes=32 << 20),
        cost_estimate=pl.CostEstimate(
            flops=heads * 8 * tokens * tokens * HEAD, bytes_accessed=8 * tokens * heads * HEAD, transcendentals=0),
    )(*args)


def body(queries, keys, values, out_weight, out_grad):
    n = lax.axis_size("seq")
    tokens, width = queries.shape
    heads = width // HEAD
    pad = HEAD + 8
    while (heads * pad) % (8 * n):
        pad += 8
    run = functools.partial(per_head, heads=heads, tokens=tokens, pad=pad)
    (part,) = run(sum_kernel, ins="tt", outs=[("s", F32)], args=(keys, values))
    entry = entering(part, n, False, 1)
    attended_grad = lax.dot_general(out_grad, out_weight, NT, preferred_element_type=F32)
    rounded, part_grad = run(
        attend_kernel, ins="tttst", outs=[("t", BF), ("s", F32)],
        args=(queries, keys, values, entry, attended_grad))
    weight_grad = lax.psum_scatter(
        lax.dot_general(rounded, out_grad, TN, preferred_element_type=F32),
        "seq", scatter_dimension=0, tiled=True)
    later = entering(part_grad, n, True, 2)
    query_grad, key_part, value_part = run(
        local_kernel, ins="tttst", outs=[("t", BF), ("t", F32), ("t", F32)],
        args=(queries, keys, values, entry, attended_grad))
    key_grad, value_grad = run(
        finish_kernel, ins="ttstt", outs=[("t", BF), ("t", BF)],
        args=(keys, values, later, key_part, value_part))
    return (query_grad, key_grad, value_grad, weight_grad)


def solution(mesh):
    rows = P(("groups", "seq"), None)
    return jax.shard_map(
        body, mesh=mesh, in_specs=(rows, rows, rows, P(), rows),
        out_specs=(rows, rows, rows, rows), check_vma=False)
```

time: 687 us -> 290 us (0.42); the launches traced: 677 us -> 289 us
  waiting for transfers between devices: 359 us -> 91.2 us
  Pallas kernels: 0 us -> 163 us
  blocking collectives: 156 us -> 0 us
  matrix products: 86.2 us -> 14 us
  other arithmetic: 49.2 us -> 0 us
    all_gather x2 -> x0, waiting for transfers between devices: 237 us -> none  [entering(): gathered = jax.tree.map(lambda a: lax.all_gather(a, axis), part)]
    pallas_call x0 -> x6, Pallas kernels: none -> 163 us  [the longest x2 115 us: entering(): pl.pallas_call(functools.partial(scan_kernel, n, reverse), out_shape=jax....]
    all_gather x2 -> x0, blocking collectives: 156 us -> none  [entering(): gathered = jax.tree.map(lambda a: lax.all_gather(a, axis), part)]
    dot_general x15 -> x2, matrix products: 79 us -> 14 us  [the longest x1 8.12 us: body(): lax.dot_general(rounded, out_grad, TN, preferred_element_type=F32)]
    add x62 -> x0, other arithmetic: 47 us -> none  [add_pair(): return (earlier[0] + later[0], earlier[1] + later[1])]
    reduce_scatter x1, waiting for transfers between devices: 123 us -> 91.2 us  [body(): lax.psum_scatter(lax.dot_general(rounded, out_grad, TN, preferred_element...]
    reshape x1 -> x0, matrix products: 7.19 us -> none  [attend_block(): return (numer / denom[:, :, None]).reshape(block_len, HEADS * HEAD)]
  transfers between devices with their start and end apart: 3 -> 1, of which waited for: 3 -> 1; matrix products, arithmetic and copies ran while one was open for 19% -> 0% of each run, Pallas kernels for 0% -> 35%
where the time goes in v1:
time: 290 us; the launch traced here: 289 us
  Pallas kernels  163 us (56%)
  waiting for transfers between devices  91.2 us (31%)
  between operations  14.2 us (5%)
  matrix products  14 us (5%)
  local copies, waits for them, and re-layouts  6.6 us (2%)
    pallas_call x2, Pallas kernels, entering(): pl.pallas_call(functools.partial(scan_kernel, n, reverse), out_shape=jax....  115 us
    reduce_scatter x1, waiting for transfers between devices, body(): lax.psum_scatter(lax.dot_general(rounded, out_grad, TN, preferred_element...  91.2 us
    pallas_call x4, Pallas kernels, per_head(): pl.pallas_call(kernel, grid=(heads,), in_specs=[spec[i] for i in ins], ou...  48 us
    dot_general x1, matrix products, body(): lax.dot_general(rounded, out_grad, TN, preferred_element_type=F32)  8.12 us
    unnamed x24, local copies, waits for them, and re-layouts  6.6 us
    dot_general x1, matrix products, body(): lax.dot_general(out_grad, out_weight, NT, preferred_element_type=F32)  5.89 us
  transfers between devices with their start and end apart: 1, of which 1 were waited for; matrix products, arithmetic and copies ran while one was open for 0% of the time, Pallas kernels for 35%

profile of v1, /device:TPU:0, one launch (start us, length us, event | category | flops | bytes accessed | tf_op | source)
XLA Modules:
  0.0 288.6 jit_solution(11652941873511161088)
XLA Ops:
  7.2 0.0 copy-start
  7.2 0.0 reduce-scatter.2.cloned.1.call-start
  7.2 0.0 copy-start.1
  7.2 1.3 copy-done.1
  8.5 0.0 copy-start.3
  8.5 1.2 copy-done.3
  9.8 4.1 %shard_map.84.x_ref = f32[2304,128]{1,0:T(8,128)S(1)} custom-call(bf16[256,2048]{1,0:T(8,128)(2,1)S(1)} %copy-done.1, bf16[256,2048]{1,0:T(8,128)(2,1)S(1)} %copy-done.3), custom_call_target="tpu_custom_call" | custom-call | flops 1073741824 | bytes 4194304 | tf_op jit(solution)/shard_map/pallas_call | solution.py:176
  13.9 44.9 %shard_map.85.e_ref = f32[2304,128]{1,0:T(8,128)S(1)} custom-call(f32[2304,128]{1,0:T(8,128)S(1)} %shard_map.84.x_ref), custom_call_target="tpu_custom_call" | custom-call | bytes 100000000 | tf_op jit(solution)/shard_map/pallas_call | solution.py:98
  58.9 0.0 copy-done
  58.9 0.0 copy-start.2
  58.9 0.0 copy-start.4
  58.9 0.0 copy-start.8
  58.9 5.9 %fusion.da_ref = f32[256,2048]{1,0:T(8,128)S(1)} fusion(bf16[256,2048]{1,0:T(8,128)(2,1)S(1)} %copy-done, bf16[2048,2048]{1,0:T(8,128)(2,1)} %param.8), kind=kOutput, calls=%fused_computation | convolution fusion | flops 2147483648 | bytes 11534336 | tf_op jit(solution)/shard_map/dot_general | solution.py:198
  64.8 0.0 copy-done.2
  64.8 0.0 copy-done.4
  64.8 0.0 copy-done.8
  64.8 0.0 copy-start.6
  64.9 13.4 %shard_map.87 = (bf16[256,2048]{1,0:T(8,128)(2,1)S(1)}, f32[2304,128]{1,0:T(8,128)S(1)}) custom-call(bf16[256,2048]{1,0:T(8,128)(2,1)S(1)} %copy-done.8, bf16[256,2048]{1,0:T(8,128)(2,1)S(1)} %copy-done.2, bf16[256,2048]{1,0:T(8,128)(2,1)S(1)} %copy-done.4, f32[2304,128]{1,0:T(8,128)S(1)} %shard_map.85.e_ref, f32[256,2048]{1,0:T(8,128)S(1)} %fusion.da_ref), custom_call_target="tpu_custom_call" | custom-call | flops 1073741824 | bytes 4194304 | tf_op jit(solution)/shard_map/pallas_call | solution.py:176
  78.3 0.0 copy-done.6
  78.3 0.0 copy-start.10
  78.3 1.0 copy-done.10
  79.3 8.1 %fusion.1 = f32[2048,2048]{1,0:T(8,128)} fusion(bf16[256,2048]{1,0:T(8,128)(2,1)S(1)} %get-tuple-element.17, bf16[256,2048]{1,0:T(8,128)(2,1)S(1)} %copy-done), kind=kOutput, calls=%fused_computation.1 | convolution fusion | flops 2147483648 | bytes 18874368 | tf_op jit(solution)/shard_map/dot_general | solution.py:203
  87.4 0.0 reduce-scatter.2.cloned.1.call-update
  87.5 0.0 copy-start.5
  87.5 0.0 copy-start.9
  87.5 0.0 copy-start.11
  87.5 1.4 copy-done.11
  88.9 69.6 %shard_map.88.g_ref = f32[2304,128]{1,0:T(8,128)S(1)} custom-call(f32[2304,128]{1,0:T(8,128)S(1)} %copy-done.11), custom_call_target="tpu_custom_call" | custom-call | bytes 100000000 | tf_op jit(solution)/shard_map/pallas_call | solution.py:98
  158.6 0.0 copy-done.5
  158.6 0.0 copy-done.9
  158.6 0.0 copy-start.7
  158.6 1.6 copy-done.7
  160.2 22.5 %shard_map.86 = (bf16[256,2048]{1,0:T(8,128)(2,1)}, f32[256,2048]{1,0:T(8,128)S(1)}, f32[256,2048]{1,0:T(8,128)S(1)}) custom-call(bf16[256,2048]{1,0:T(8,128)(2,1)S(1)} %copy-done.9, bf16[256,2048]{1,0:T(8,128)(2,1)S(1)} %copy-done.2, bf16[256,2048]{1,0:T(8,128)(2,1)S(1)} %copy-done.5, f32[2304,128]{1,0:T(8,128)S(1)} %shard_map.85.e_ref, ...), custom_call_target="tpu_custom_call" | custom-call | flops 1073741824 | bytes 4194304 | tf_op jit(solution)/shard_map/pallas_call | solution.py:176
  182.7 7.9 %shard_map.89 = (bf16[256,2048]{1,0:T(8,128)(2,1)}, bf16[256,2048]{1,0:T(8,128)(2,1)}) custom-call(bf16[256,2048]{1,0:T(8,128)(2,1)S(1)} %copy-done.2, bf16[256,2048]{1,0:T(8,128)(2,1)S(1)} %copy-done.5, f32[2304,128]{1,0:T(8,128)S(1)} %shard_map.88.g_ref, f32[256,2048]{1,0:T(8,128)S(1)} %get-tuple-element.13.dk_ref, f32[256,2048]{1,0:T(8,128)S(1)} %get-tuple-element.14.dv_ref), custom_call_target="tpu_custom_call" | custom-call | flops 1073741824 | bytes 4194304 | tf_op jit(solution)/shard_map/pallas_call | solution.py:176
  190.6 91.2 %reduce-scatter.2.cloned.1.call-done = f32[64,2048]{1,0:T(8,128)} async-done(((f32[2048,2048]{1,0:T(8,128)}), f32[64,2048]{1,0:T(8,128)}) %reduce-scatter.2.cloned.1.call-update) | async-done | bytes 524304 | tf_op jit(solution)/shard_map/reduce_scatter | solution.py:202
Async XLA Ops:
  7.2 51.7 %copy-start = (bf16[256,2048]{1,0:T(8,128)(2,1)S(1)}, bf16[256,2048]{1,0:T(8,128)(2,1)}, u32[]{:S(2)}) copy-start(bf16[256,2048]{1,0:T(8,128)(2,1)} %param.9) | copy-start | bytes 3145732
  7.2 274.6 %reduce-scatter.2.cloned.1.call-start = ((), (), s32[]{:S(2)}) async-start(), calls=%async_computation.1 | async-start | bytes 17301504 | tf_op jit(solution)/shard_map/reduce_scatter | solution.py:202
  7.2 1.3 copy-start.1
  8.5 1.2 copy-start.3
  58.9 5.9 %copy-start.2 = (bf16[256,2048]{1,0:T(8,128)(2,1)S(1)}, bf16[256,2048]{1,0:T(8,128)(2,1)}, u32[]{:S(2)}) copy-start(bf16[256,2048]{1,0:T(8,128)(2,1)} %k_ref.7) | copy-start | bytes 3145732
  58.9 5.9 %copy-start.4 = (bf16[256,2048]{1,0:T(8,128)(2,1)S(1)}, bf16[256,2048]{1,0:T(8,128)(2,1)}, u32[]{:S(2)}) copy-start(bf16[256,2048]{1,0:T(8,128)(2,1)} %v_ref.7) | copy-start | bytes 3145732
  58.9 5.9 %copy-start.8 = (bf16[256,2048]{1,0:T(8,128)(2,1)S(1)}, bf16[256,2048]{1,0:T(8,128)(2,1)}, u32[]{:S(2)}) copy-start(bf16[256,2048]{1,0:T(8,128)(2,1)} %q_ref.3) | copy-start | bytes 3145732
  64.8 13.4 %copy-start.6 = (f32[256,2048]{1,0:T(8,128)}, f32[256,2048]{1,0:T(8,128)S(1)}, u32[]{:S(2)}) copy-start(f32[256,2048]{1,0:T(8,128)S(1)} %fusion.da_ref) | copy-start | bytes 6291460
  78.3 1.0 copy-start.10
  87.5 71.1 %copy-start.5 = (bf16[256,2048]{1,0:T(8,128)(2,1)S(1)}, bf16[256,2048]{1,0:T(8,128)(2,1)}, u32[]{:S(2)}) copy-start(bf16[256,2048]{1,0:T(8,128)(2,1)} %v_ref.7) | copy-start | bytes 3145732
  87.5 71.1 %copy-start.9 = (bf16[256,2048]{1,0:T(8,128)(2,1)S(1)}, bf16[256,2048]{1,0:T(8,128)(2,1)}, u32[]{:S(2)}) copy-start(bf16[256,2048]{1,0:T(8,128)(2,1)} %q_ref.3) | copy-start | bytes 3145732
  87.5 1.4 copy-start.11
  158.6 1.6 copy-start.7
Sparse Core Ops, SparseCore 0:
  87.6 194.1 reduce-scatter.1

commit v2 on v1

--- a/solution.py
+++ b/solution.py
@@ -45,16 +45,12 @@
     return me + (1 - 2 * ((me // (1 << k)) % 2)) * (1 << k)
 
 
-def scan_kernel(n, reverse, x_ref, e_ref, tot, recv, near, out, su, ru, sd, rd):
+def sweep_up(n, reverse, x_ref, tot, recv, near, su, ru):
     me = lax.axis_index("seq")
-    levels = bits_of(n)
     rows = x_ref.shape[0]
-    barrier = pltpu.get_barrier_semaphore()
-    for k in range(levels):
-        pl.semaphore_signal(barrier, inc=1, device_id={"seq": partner_of(me, k)}, device_id_type=MESH)
-    pl.semaphore_wait(barrier, levels)
     base = 0
     keeps = []
+    levels = bits_of(n)
     for k in range(levels):
         half = rows >> (k + 1)
         off = rows - (rows >> k)
@@ -62,22 +58,27 @@
         keep = pl.multiple_of(base + bit * half, 8)
         give = pl.multiple_of(base + (1 - bit) * half, 8)
         src = x_ref if k == 0 else tot
-        buf = recv.at[pl.ds(off, half)]
         copy = pltpu.make_async_remote_copy(
-            src_ref=src.at[pl.ds(give, half)], dst_ref=buf, send_sem=su.at[k], recv_sem=ru.at[k],
+            src_ref=src.at[pl.ds(give, half)], dst_ref=recv.at[pl.ds(off, half)],
+            send_sem=su.at[k], recv_sem=ru.at[k],
             device_id={"seq": partner_of(me, k)}, device_id_type=MESH)
         copy.start()
         copy.wait()
         mine = src[pl.ds(keep, half), :]
         theirs = recv[pl.ds(off, half), :]
-        first = jnp.where(bit == (1 if reverse else 0), mine, theirs)
-        near[pl.ds(off, half), :] = first
+        near[pl.ds(off, half), :] = jnp.where(bit == (1 if reverse else 0), mine, theirs)
         if k + 1 < levels:
             tot[pl.ds(keep, half), :] = mine + theirs
         keeps.append((keep, half, off, bit))
         base = keep
-    e_ref[pl.ds(base, rows >> levels), :] = jnp.zeros((rows >> levels, x_ref.shape[1]), F32)
-    for k in reversed(range(levels)):
+    return keeps
+
+
+def sweep_down(keeps, reverse, e_ref, near, out, sd, rd):
+    me = lax.axis_index("seq")
+    keep, half, _, _ = keeps[-1]
+    e_ref[pl.ds(keep, half), :] = jnp.zeros((half, e_ref.shape[1]), F32)
+    for k in reversed(range(len(keeps))):
         keep, half, off, bit = keeps[k]
         early = bit == (1 if reverse else 0)
         now = e_ref[pl.ds(keep, half), :]
@@ -92,19 +93,112 @@
         copy.wait()
 
 
-def entering(x, n, reverse, collective_id):
-    levels = bits_of(n)
-    rows, cols = x.shape
+def greet(peers):
+    barrier = pltpu.get_barrier_semaphore()
+    for peer in peers:
+        pl.semaphore_signal(barrier, inc=1, device_id={"seq": peer}, device_id_type=MESH)
+    pl.semaphore_wait(barrier, len(peers))
+
+
+def scan_kernel(n, x_ref, e_ref, tot, recv, near, out, su, ru, sd, rd):
+    me = lax.axis_index("seq")
+    greet([partner_of(me, k) for k in range(bits_of(n))])
+    keeps = sweep_up(n, False, x_ref, tot, recv, near, su, ru)
+    sweep_down(keeps, False, e_ref, near, out, sd, rd)
+
+
+def scan_scratch(n, shape):
+    return [pltpu.VMEM(shape, F32)] * 4 + [pltpu.SemaphoreType.DMA((bits_of(n),))] * 4
+
+
+def entering(x, n):
     return pl.pallas_call(
-        functools.partial(scan_kernel, n, reverse),
+        functools.partial(scan_kernel, n),
         out_shape=jax.ShapeDtypeStruct(x.shape, F32),
         in_specs=[pl.BlockSpec(memory_space=pltpu.VMEM)],
         out_specs=pl.BlockSpec(memory_space=pltpu.VMEM),
-        scratch_shapes=[pltpu.VMEM((rows, cols), F32)] * 4 + [pltpu.SemaphoreType.DMA((levels,))] * 4,
+        scratch_shapes=scan_scratch(n, x.shape),
         compiler_params=pltpu.CompilerParams(
-            collective_id=collective_id, has_side_effects=True, vmem_limit_bytes=24 << 20),
+            collective_id=1, has_side_effects=True, vmem_limit_bytes=24 << 20),
         cost_estimate=pl.CostEstimate(flops=0, bytes_accessed=100_000_000, transcendentals=0),
     )(x)
+
+
+def grads_kernel(n, plane, x_ref, r_ref, og_ref, e_ref, w_ref, tot, recv, near, out, su, ru, sd, rd,
+                 og, rt, part, zr, so, sp, rp, sz, rz):
+    me = lax.axis_index("seq")
+    layers = n // plane
+    spot, layer = me % plane, me // plane
+    tokens = r_ref.shape[3]
+    load = pltpu.make_async_copy(og_ref, og, so)
+    load.start()
+    near_peers = [layer * plane + (spot + j) % plane for j in range(1, plane)]
+    far_peers = [((layer + j) % layers) * plane + spot for j in range(1, layers)]
+    greet(near_peers + far_peers)
+    swaps = []
+    for j in range(1, plane):
+        copy = pltpu.make_async_remote_copy(
+            src_ref=r_ref.at[:, (spot + j) % plane], dst_ref=rt.at[j],
+            send_sem=sp.at[j], recv_sem=rp.at[j],
+            device_id={"seq": near_peers[j - 1]}, device_id_type=MESH)
+        copy.start()
+        swaps.append(copy)
+    keeps = sweep_up(n, True, x_ref, tot, recv, near, su, ru)
+    rt[0] = r_ref[:, spot]
+    load.wait()
+    for copy in swaps:
+        copy.wait()
+    step = 512
+
+    def columns(c, carry):
+        cols = pl.ds(pl.multiple_of(c * step, step), step)
+        acc = None
+        for j in range(plane):
+            rows = pl.ds(pl.multiple_of(((spot - j + plane) % plane) * tokens, tokens), tokens)
+            left = rt[j].reshape(layers * rt.shape[2], tokens).astype(BF)
+            term = lax.dot_general(left, og[rows, cols].astype(BF), NN, preferred_element_type=F32)
+            acc = term if acc is None else acc + term
+        part[:, :, cols] = acc.reshape(layers, rt.shape[2], step)
+        return carry
+
+    lax.fori_loop(0, og.shape[1] // step, columns, 0)
+    sums = []
+    for j in range(1, layers):
+        copy = pltpu.make_async_remote_copy(
+            src_ref=part.at[(layer + j) % layers], dst_ref=zr.at[j],
+            send_sem=sz.at[j], recv_sem=rz.at[j],
+            device_id={"seq": far_peers[j - 1]}, device_id_type=MESH)
+        copy.start()
+        sums.append(copy)
+    sweep_down(keeps, True, e_ref, near, out, sd, rd)
+    for copy in sums:
+        copy.wait()
+    total = part[layer]
+    for j in range(1, layers):
+        total = total + zr[j]
+    w_ref[...] = total
+
+
+def gradients(x, turned, og, n, plane):
+    layers = n // plane
+    rows, tokens = turned.shape
+    width = og.shape[1]
+    mine = rows // n
+    vm = pl.BlockSpec(memory_space=pltpu.VMEM)
+    dma = pltpu.SemaphoreType.DMA
+    return pl.pallas_call(
+        functools.partial(grads_kernel, n, plane),
+        out_shape=[jax.ShapeDtypeStruct(x.shape, F32), jax.ShapeDtypeStruct((mine, width), F32)],
+        in_specs=[vm, vm, pl.BlockSpec(memory_space=pl.ANY)],
+        out_specs=[vm, vm],
+        scratch_shapes=scan_scratch(n, x.shape) + [
+            pltpu.VMEM(og.shape, F32), pltpu.VMEM((plane, layers, mine, tokens), F32),
+            pltpu.VMEM((layers, mine, width), F32), pltpu.VMEM((layers, mine, width), F32),
+            dma, dma((plane,)), dma((plane,)), dma((layers,)), dma((layers,))],
+        compiler_params=pltpu.CompilerParams(
+            collective_id=2, has_side_effects=True, vmem_limit_bytes=48 << 20),
+        cost_estimate=pl.CostEstimate(flops=0, bytes_accessed=200_000_000, transcendentals=0),
+    )(x, turned.reshape(layers, plane, mine, tokens), og)
 
 
 def features(x):
@@ -140,7 +234,7 @@
 
 def attend_kernel(q_ref, k_ref, v_ref, e_ref, da_ref, r_ref, g_ref):
     fq, fq_s, _, _, _, _, _, inv, att = forward_of(q_ref[...], k_ref[...], v_ref[...], e_ref[...])
-    r_ref[...] = att.astype(BF)
+    r_ref[...] = att.T
     dn = da_ref[...] * inv
     dden = -jnp.sum(dn * att, axis=1, keepdims=True)
     g_ref[...] = with_row(mm(dn, fq_s, TN), jnp.sum(fq * dden, axis=0, keepdims=True), g_ref.shape[0])
@@ -171,8 +265,9 @@
     spec = {
         "t": pl.BlockSpec((tokens, HEAD), lambda h: (0, h)),
         "s": pl.BlockSpec((pad, HEAD), lambda h: (h, 0)),
+        "r": pl.BlockSpec((HEAD, tokens), lambda h: (h, 0)),
     }
-    shape = {"t": (tokens, heads * HEAD), "s": (heads * pad, HEAD)}
+    shape = {"t": (tokens, heads * HEAD), "s": (heads * pad, HEAD), "r": (heads * HEAD, tokens)}
     return pl.pallas_call(
         kernel,
         grid=(heads,),
@@ -193,19 +288,19 @@
     while (heads * pad) % (8 * n):
         pad += 8
     run = functools.partial(per_head, heads=heads, tokens=tokens, pad=pad)
+    plane = min(8, n)
+    blocks = [list(range(at, at + plane)) for at in range(0, n, plane)]
+    gathered = lax.all_gather(out_grad.astype(F32), "seq", axis_index_groups=blocks, tiled=True)
     (part,) = run(sum_kernel, ins="tt", outs=[("s", F32)], args=(keys, values))
-    entry = entering(part, n, False, 1)
+    entry = entering(part, n)
     attended_grad = lax.dot_general(out_grad, out_weight, NT, preferred_element_type=F32)
-    rounded, part_grad = run(
-        attend_kernel, ins="tttst", outs=[("t", BF), ("s", F32)],
+    turned, part_grad = run(
+        attend_kernel, ins="tttst", outs=[("r", F32), ("s", F32)],
         args=(queries, keys, values, entry, attended_grad))
-    weight_grad = lax.psum_scatter(
-        lax.dot_general(rounded, out_grad, TN, preferred_element_type=F32),
-        "seq", scatter_dimension=0, tiled=True)
-    later = entering(part_grad, n, True, 2)
     query_grad, key_part, value_part = run(
         local_kernel, ins="tttst", outs=[("t", BF), ("t", F32), ("t", F32)],
         args=(queries, keys, values, entry, attended_grad))
+    later, weight_grad = gradients(part_grad, turned, gathered, n, plane)
     key_grad, value_grad = run(
         finish_kernel, ins="ttstt", outs=[("t", BF), ("t", BF)],
         args=(keys, values, later, key_part, value_part))

time: 290 us -> 251 us (0.87)
  waiting for transfers between devices: 91.2 us -> 0.02 us
  Pallas kernels: 163 us -> 221 us
  matrix products: 14 us -> 5.92 us
  other arithmetic: 0 us -> 2.94 us
    reduce_scatter x1 -> x0, waiting for transfers between devices: 91.2 us -> none  [body(): lax.psum_scatter(lax.dot_general(rounded, out_grad, TN, preferred_element...]
    pallas_call x2, Pallas kernels: 115 us -> 172 us  [the longest x1 111 us: gradients(): pl.pallas_call(functools.partial(grads_kernel, n, plane), out_shape=[jax....]
    dot_general x1 -> x0, matrix products: 8.12 us -> none  [body(): lax.dot_general(rounded, out_grad, TN, preferred_element_type=F32)]
    convert_element_type x0 -> x1, other arithmetic: none -> 2.94 us  [body(): out_grad.astype(F32)]
    unnamed x24 -> x21, local copies, waits for them, and re-layouts: 6.6 us -> 6.44 us
  transfers between devices with their start and end apart: 1 -> 1, of which waited for: 1 -> 0; matrix products, arithmetic and copies ran while one was open for 0% -> 2% of each run, Pallas kernels for 35% -> 41%
where the time goes in v2:
time: 251 us
  Pallas kernels  221 us (88%)
  between operations  14.2 us (6%)
  local copies, waits for them, and re-layouts  6.44 us (3%)
  matrix products  5.92 us (2%)
  other arithmetic  2.94 us (1%)
    pallas_call x1, Pallas kernels, gradients(): pl.pallas_call(functools.partial(grads_kernel, n, plane), out_shape=[jax....  111 us
    pallas_call x1, Pallas kernels, entering(): pl.pallas_call(functools.partial(scan_kernel, n), out_shape=jax.ShapeDtyp...  61.4 us
    pallas_call x4, Pallas kernels, per_head(): pl.pallas_call(kernel, grid=(heads,), in_specs=[spec[i] for i in ins], ou...  49 us
    unnamed x21, local copies, waits for them, and re-layouts  6.44 us
    dot_general x1, matrix products, body(): lax.dot_general(out_grad, out_weight, NT, preferred_element_type=F32)  5.92 us
  transfers between devices with their start and end apart: 1, of which 0 were waited for; matrix products, arithmetic and copies ran while one was open for 2% of the time, Pallas kernels for 41%

profile of v2, /device:TPU:0, one launch (start us, length us, event | category | flops | bytes accessed | tf_op | source)
XLA Modules:
  0.0 250.9 jit_solution(4925332494727621235)
XLA Ops:
  7.2 0.0 copy-start.1
  7.2 0.0 copy-start
  7.2 0.0 all-gather.2.cloned.1.call-start
  7.2 2.9 %convert_element_type.3 = f32[256,2048]{1,0:T(8,128)} convert(bf16[256,2048]{1,0:T(8,128)(2,1)} %param.9) | non-fusion elementwise | flops 524288 | bytes 3145728 | tf_op jit(solution)/shard_map/convert_element_type | solution.py:293
  10.2 0.0 all-gather.2.cloned.1.call-update
  10.2 0.0 copy-done.1
  10.2 0.0 copy-done
  10.2 4.2 %shard_map.84.x_ref = f32[2304,128]{1,0:T(8,128)S(1)} custom-call(bf16[256,2048]{1,0:T(8,128)(2,1)S(1)} %copy-done, bf16[256,2048]{1,0:T(8,128)(2,1)S(1)} %copy-done.1), custom_call_target="tpu_custom_call" | custom-call | flops 1073741824 | bytes 4194304 | tf_op jit(solution)/shard_map/pallas_call | solution.py:271
  14.4 0.0 copy-start.9
  14.4 61.4 %shard_map.85.e_ref = f32[2304,128]{1,0:T(8,128)S(1)} custom-call(f32[2304,128]{1,0:T(8,128)S(1)} %shard_map.84.x_ref), custom_call_target="tpu_custom_call" | custom-call | bytes 100000000 | tf_op jit(solution)/shard_map/pallas_call | solution.py:115
  75.8 0.0 copy-done.9
  75.8 0.0 copy-start.2
  75.8 5.9 %fusion.da_ref = f32[256,2048]{1,0:T(8,128)S(1)} fusion(bf16[256,2048]{1,0:T(8,128)(2,1)S(1)} %copy-done.9, bf16[2048,2048]{1,0:T(8,128)(2,1)} %param.8), kind=kOutput, calls=%fused_computation | convolution fusion | flops 2147483648 | bytes 11534336 | tf_op jit(solution)/shard_map/dot_general | solution.py:296
  81.7 0.0 copy-done.2
  81.7 14.4 %shard_map.87 = (f32[2048,256]{1,0:T(8,128)S(1)}, f32[2304,128]{1,0:T(8,128)S(1)}) custom-call(bf16[256,2048]{1,0:T(8,128)(2,1)S(1)} %copy-done.2, bf16[256,2048]{1,0:T(8,128)(2,1)S(1)} %copy-done, bf16[256,2048]{1,0:T(8,128)(2,1)S(1)} %copy-done.1, f32[2304,128]{1,0:T(8,128)S(1)} %shard_map.85.e_ref, f32[256,2048]{1,0:T(8,128)S(1)} %fusion.da_ref), custom_call_target="tpu_custom_call" | custom-call | flops 1073741824 | bytes 4194304 | tf_op jit(solution)/shard_map/pallas_call | solution.py:271
  96.1 0.0 copy-start.7
  96.2 1.3 copy-done.7
  97.5 22.5 %shard_map.86 = (bf16[256,2048]{1,0:T(8,128)(2,1)}, f32[256,2048]{1,0:T(8,128)S(1)}, f32[256,2048]{1,0:T(8,128)S(1)}) custom-call(bf16[256,2048]{1,0:T(8,128)(2,1)S(1)} %copy-done.2, bf16[256,2048]{1,0:T(8,128)(2,1)S(1)} %copy-done, bf16[256,2048]{1,0:T(8,128)(2,1)S(1)} %copy-done.1, f32[2304,128]{1,0:T(8,128)S(1)} %shard_map.85.e_ref, ...), custom_call_target="tpu_custom_call" | custom-call | flops 1073741824 | bytes 4194304 | tf_op jit(solution)/shard_map/pallas_call | solution.py:271
  120.0 0.0 copy-start.3
  120.0 1.3 copy-done.3
  121.4 0.0 copy-start.5
  121.4 1.4 copy-done.5
  122.7 0.0 all-gather.2.cloned.1.call-done.og_ref
  122.7 0.0 copy-start.8
  122.7 1.6 copy-done.8
  124.3 0.0 copy-start.4
  124.3 0.0 copy-start.6
  124.3 111.0 %shard_map.88 = (f32[2304,128]{1,0:T(8,128)S(1)}, f32[64,2048]{1,0:T(8,128)S(1)}) custom-call(f32[2304,128]{1,0:T(8,128)S(1)} %get-tuple-element.14.x_ref, f32[4,8,64,256]{3,2,1,0:T(8,128)S(1)} %bitcast.3, f32[2048,2048]{1,0:T(8,128)} %all-gather.2.cloned.1.call-done.og_ref), custom_call_target="tpu_custom_call" | custom-call | bytes 200000000 | tf_op jit(solution)/shard_map/pallas_call | solution.py:189
  235.3 0.0 copy-done.4
  235.3 0.0 copy-done.6
  235.3 7.9 %shard_map.89 = (bf16[256,2048]{1,0:T(8,128)(2,1)}, bf16[256,2048]{1,0:T(8,128)(2,1)}) custom-call(bf16[256,2048]{1,0:T(8,128)(2,1)S(1)} %copy-done, bf16[256,2048]{1,0:T(8,128)(2,1)S(1)} %copy-done.1, f32[2304,128]{1,0:T(8,128)S(1)} %get-tuple-element.16.g_ref, f32[256,2048]{1,0:T(8,128)S(1)} %copy-done.4, f32[256,2048]{1,0:T(8,128)S(1)} %copy-done.6), custom_call_target="tpu_custom_call" | custom-call | flops 1073741824 | bytes 4194304 | tf_op jit(solution)/shard_map/pallas_call | solution.py:271
  243.3 0.8 copy.10
Async XLA Ops:
  7.2 3.0 %copy-start.1 = (bf16[256,2048]{1,0:T(8,128)(2,1)S(1)}, bf16[256,2048]{1,0:T(8,128)(2,1)}, u32[]{:S(2)}) copy-start(bf16[256,2048]{1,0:T(8,128)(2,1)} %v_ref.7) | copy-start | bytes 3145732
  7.2 3.0 %copy-start = (bf16[256,2048]{1,0:T(8,128)(2,1)S(1)}, bf16[256,2048]{1,0:T(8,128)(2,1)}, u32[]{:S(2)}) copy-start(bf16[256,2048]{1,0:T(8,128)(2,1)} %k_ref.7) | copy-start | bytes 3145732
  7.2 115.5 %all-gather.2.cloned.1.call-start = ((), (), s32[]{:S(2)}) async-start(), calls=%async_computation | async-start | bytes 18874368 | tf_op jit(solution)/shard_map/all_gather | solution.py:293
  14.4 61.4 %copy-start.9 = (bf16[256,2048]{1,0:T(8,128)(2,1)S(1)}, bf16[256,2048]{1,0:T(8,128)(2,1)}, u32[]{:S(2)}) copy-start(bf16[256,2048]{1,0:T(8,128)(2,1)} %param.9) | copy-start | bytes 3145732
  75.8 5.9 %copy-start.2 = (bf16[256,2048]{1,0:T(8,128)(2,1)S(1)}, bf16[256,2048]{1,0:T(8,128)(2,1)}, u32[]{:S(2)}) copy-start(bf16[256,2048]{1,0:T(8,128)(2,1)} %q_ref.3) | copy-start | bytes 3145732
  96.1 1.4 copy-start.7
  120.0 1.3 copy-start.3
  121.4 1.4 copy-start.5
  122.7 1.6 copy-start.8
  124.3 111.0 %copy-start.4 = (f32[256,2048]{1,0:T(8,128)S(1)}, f32[256,2048]{1,0:T(8,128)}, u32[]{:S(2)}) copy-start(f32[256,2048]{1,0:T(8,128)} %copy-done.3) | copy-start | bytes 6291460
  124.3 111.0 %copy-start.6 = (f32[256,2048]{1,0:T(8,128)S(1)}, f32[256,2048]{1,0:T(8,128)}, u32[]{:S(2)}) copy-start(f32[256,2048]{1,0:T(8,128)} %copy-done.5) | copy-start | bytes 6291460
Sparse Core Ops, SparseCore 0:
  10.3 100.0 all-gather.1

commit v3 on v2

--- a/solution.py
+++ b/solution.py
@@ -74,11 +74,12 @@
     return keeps
 
 
-def sweep_down(keeps, reverse, e_ref, near, out, sd, rd):
+def sweep_down(keeps, bits, reverse, e_ref, near, out, sd, rd):
     me = lax.axis_index("seq")
-    keep, half, _, _ = keeps[-1]
-    e_ref[pl.ds(keep, half), :] = jnp.zeros((half, e_ref.shape[1]), F32)
-    for k in reversed(range(len(keeps))):
+    if len(keeps) - 1 in bits:
+        keep, half, _, _ = keeps[-1]
+        e_ref[pl.ds(keep, half), :] = jnp.zeros((half, e_ref.shape[1]), F32)
+    for k in reversed(bits):
         keep, half, off, bit = keeps[k]
         early = bit == (1 if reverse else 0)
         now = e_ref[pl.ds(keep, half), :]
@@ -104,7 +105,7 @@
     me = lax.axis_index("seq")
     greet([partner_of(me, k) for k in range(bits_of(n))])
     keeps = sweep_up(n, False, x_ref, tot, recv, near, su, ru)
-    sweep_down(keeps, False, e_ref, near, out, sd, rd)
+    sweep_down(keeps, range(len(keeps)), False, e_ref, near, out, sd, rd)
 
 
 def scan_scratch(n, shape):
@@ -124,8 +125,9 @@
     )(x)
 
 
-def grads_kernel(n, plane, x_ref, r_ref, og_ref, e_ref, w_ref, tot, recv, near, out, su, ru, sd, rd,
-                 og, rt, part, zr, so, sp, rp, sz, rz):
+def grads_kernel(n, plane, x_ref, r_ref, og_ref, q_ref, k_ref, v_ref, en_ref, da_ref,
+                 dq_ref, dk_ref, dv_ref, w_ref, tot, recv, near, out, su, ru, sd, rd,
+                 e_ref, og, rt, part, zr, so, sp, rp, sz, rz):
     me = lax.axis_index("seq")
     layers = n // plane
     spot, layer = me % plane, me // plane
@@ -162,6 +164,8 @@
         return carry
 
     lax.fori_loop(0, og.shape[1] // step, columns, 0)
+    low = bits_of(plane)
+    sweep_down(keeps, range(low, len(keeps)), True, e_ref, near, out, sd, rd)
     sums = []
     for j in range(1, layers):
         copy = pltpu.make_async_remote_copy(
@@ -170,7 +174,18 @@
             device_id={"seq": far_peers[j - 1]}, device_id_type=MESH)
         copy.start()
         sums.append(copy)
-    sweep_down(keeps, True, e_ref, near, out, sd, rd)
+    sweep_down(keeps, range(low), True, e_ref, near, out, sd, rd)
+    heads = q_ref.shape[1] // HEAD
+    pad = x_ref.shape[0] // heads
+
+    def head(h, carry):
+        cols = pl.ds(pl.multiple_of(h * HEAD, HEAD), HEAD)
+        block = pl.ds(pl.multiple_of(h * pad, 8), pad)
+        dq_ref[:, cols], dk_ref[:, cols], dv_ref[:, cols] = gradients_of(
+            q_ref[:, cols], k_ref[:, cols], v_ref[:, cols], en_ref[block, :], da_ref[:, cols], e_ref[block, :])
+        return carry
+
+    lax.fori_loop(0, heads, head, 0)
     for copy in sums:
         copy.wait()
     total = part[layer]
@@ -179,7 +194,7 @@
     w_ref[...] = total
 
 
-def gradients(x, turned, og, n, plane):
+def gradients(x, turned, og, queries, keys, values, entry, attended_grad, n, plane):
     layers = n // plane
     rows, tokens = turned.shape
     width = og.shape[1]
@@ -188,17 +203,18 @@
     dma = pltpu.SemaphoreType.DMA
     return pl.pallas_call(
         functools.partial(grads_kernel, n, plane),
-        out_shape=[jax.ShapeDtypeStruct(x.shape, F32), jax.ShapeDtypeStruct((mine, width), F32)],
-        in_specs=[vm, vm, pl.BlockSpec(memory_space=pl.ANY)],
-        out_specs=[vm, vm],
+        out_shape=[jax.ShapeDtypeStruct(queries.shape, BF)] * 3 + [jax.ShapeDtypeStruct((mine, width), F32)],
+        in_specs=[vm, vm, pl.BlockSpec(memory_space=pl.ANY)] + [vm] * 5,
+        out_specs=[vm] * 4,
         scratch_shapes=scan_scratch(n, x.shape) + [
+            pltpu.VMEM(x.shape, F32),
             pltpu.VMEM(og.shape, F32), pltpu.VMEM((plane, layers, mine, tokens), F32),
             pltpu.VMEM((layers, mine, width), F32), pltpu.VMEM((layers, mine, width), F32),
             dma, dma((plane,)), dma((plane,)), dma((layers,)), dma((layers,))],
         compiler_params=pltpu.CompilerParams(
             collective_id=2, has_side_effects=True, vmem_limit_bytes=48 << 20),
         cost_estimate=pl.CostEstimate(flops=0, bytes_accessed=200_000_000, transcendentals=0),
-    )(x, turned.reshape(layers, plane, mine, tokens), og)
+    )(x, turned.reshape(layers, plane, mine, tokens), og, queries, keys, values, entry, attended_grad)
 
 
 def features(x):
@@ -240,25 +256,18 @@
     g_ref[...] = with_row(mm(dn, fq_s, TN), jnp.sum(fq * dden, axis=0, keepdims=True), g_ref.shape[0])
 
 
-def local_kernel(q_ref, k_ref, v_ref, e_ref, da_ref, dq_ref, dk_ref, dv_ref):
-    v = v_ref[...]
-    fq, fq_s, qslope, fk_s, causal, scores, z, inv, att = forward_of(q_ref[...], k_ref[...], v, e_ref[...])
-    dn = da_ref[...] * inv
+def gradients_of(q, k, v, entry, da, later):
+    fq, fq_s, qslope, fk_s, causal, scores, z, inv, att = forward_of(q, k, v, entry)
+    kslope = jnp.where(k.astype(F32) > 0, 1.0, jnp.exp(jnp.minimum(k.astype(F32), 0.0)))
+    dn = da * inv
     dden = -jnp.sum(dn * att, axis=1, keepdims=True)
-    dn_b = split(dn)
-    dp = split(jnp.where(causal, mm(dn_b, v, NT) + dden, 0.0))
-    dfq = mm(dp, fk_s, NN) + mm(dn_b, e_ref[:HEAD, :], NN) + dden * z
-    dq_ref[...] = (dfq * qslope).astype(BF)
-    dk_ref[...] = mm(dp, fq_s, TN)
-    dv_ref[...] = mm(scores, dn_b, TN)
-
-
-def finish_kernel(k_ref, v_ref, g_ref, dk_ref, dv_ref, ok_ref, ov_ref):
-    fk, kslope = features(k_ref[...])
-    g = split(g_ref[:HEAD, :])
-    dfk = dk_ref[...] + mm(v_ref[...], g, NN) + g_ref[HEAD:HEAD + 1, :]
-    ok_ref[...] = (dfk * kslope).astype(BF)
-    ov_ref[...] = (dv_ref[...] + mm(fk, g, NT)).astype(BF)
+    dn_s = split(dn)
+    dp = split(jnp.where(causal, mm(dn_s, v, NT) + dden, 0.0))
+    g = split(later[:HEAD, :])
+    dfq = mm(dp, fk_s, NN) + mm(dn_s, entry[:HEAD, :], NN) + dden * z
+    dfk = mm(dp, fq_s, TN) + mm(v, g, NN) + later[HEAD:HEAD + 1, :]
+    dv = mm(scores, dn_s, TN) + mm(fk_s, g, NT)
+    return (dfq * qslope).astype(BF), (dfk * kslope).astype(BF), dv.astype(BF)
 
 
 def per_head(kernel, heads, tokens, pad, ins, outs, args):
@@ -297,13 +306,8 @@
     turned, part_grad = run(
         attend_kernel, ins="tttst", outs=[("r", F32), ("s", F32)],
         args=(queries, keys, values, entry, attended_grad))
-    query_grad, key_part, value_part = run(
-        local_kernel, ins="tttst", outs=[("t", BF), ("t", F32), ("t", F32)],
-        args=(queries, keys, values, entry, attended_grad))
-    later, weight_grad = gradients(part_grad, turned, gathered, n, plane)
-    key_grad, value_grad = run(
-        finish_kernel, ins="ttstt", outs=[("t", BF), ("t", BF)],
-        args=(keys, values, later, key_part, value_part))
+    query_grad, key_grad, value_grad, weight_grad = gradients(
+        part_grad, turned, gathered, queries, keys, values, entry, attended_grad, n, plane)
     return (query_grad, key_grad, value_grad, weight_grad)
 
 

time: 251 us -> 224 us (0.89)
  Pallas kernels: 221 us -> 181 us
  waiting for transfers between devices: 0.02 us -> 11.4 us
    pallas_call x4 -> x2, Pallas kernels: 49 us -> 18.6 us  [per_head(): pl.pallas_call(kernel, grid=(heads,), in_specs=[spec[i] for i in ins], ou...]
    all_gather x1, waiting for transfers between devices: 0.01 us -> 11.4 us  [body(): lax.all_gather(out_grad.astype(F32), 'seq', axis_index_groups=blocks, til...]
    pallas_call x1, Pallas kernels: 111 us -> 101 us  [gradients(): pl.pallas_call(functools.partial(grads_kernel, n, plane), out_shape=[jax....]
    unnamed x21 -> x28, local copies, waits for them, and re-layouts: 6.44 us -> 8.54 us
  transfers between devices with their start and end apart: 1 -> 1, of which waited for: 0 -> 1; matrix products, arithmetic and copies ran while one was open for 2% -> 3% of each run, Pallas kernels for 41% -> 36%
where the time goes in v3:
time: 224 us
  Pallas kernels  181 us (81%)
  between operations  14.2 us (6%)
  waiting for transfers between devices  11.4 us (5%)
  local copies, waits for them, and re-layouts  8.54 us (4%)
  matrix products  6.28 us (3%)
  other arithmetic  2.94 us (1%)
    pallas_call x1, Pallas kernels, gradients(): pl.pallas_call(functools.partial(grads_kernel, n, plane), out_shape=[jax....  101 us
    pallas_call x1, Pallas kernels, entering(): pl.pallas_call(functools.partial(scan_kernel, n), out_shape=jax.ShapeDtyp...  61.4 us
    pallas_call x2, Pallas kernels, per_head(): pl.pallas_call(kernel, grid=(heads,), in_specs=[spec[i] for i in ins], ou...  18.6 us
    all_gather x1, waiting for transfers between devices, body(): lax.all_gather(out_grad.astype(F32), 'seq', axis_index_groups=blocks, til...  11.4 us
    unnamed x28, local copies, waits for them, and re-layouts  8.54 us
    dot_general x1, matrix products, body(): lax.dot_general(out_grad, out_weight, NT, preferred_element_type=F32)  6.28 us
  transfers between devices with their start and end apart: 1, of which 1 were waited for; matrix products, arithmetic and copies ran while one was open for 3% of the time, Pallas kernels for 36%

profile of v3, /device:TPU:0, one launch (start us, length us, event | category | flops | bytes accessed | tf_op | source)
XLA Modules:
  0.0 224.0 jit_solution(6641753432335234959)
XLA Ops:
  7.2 0.0 copy-start.7
  7.2 0.0 copy-start.4
  7.2 0.0 all-gather.2.cloned.1.call-start
  7.2 2.9 %convert_element_type.3 = f32[256,2048]{1,0:T(8,128)} convert(bf16[256,2048]{1,0:T(8,128)(2,1)} %param.9) | non-fusion elementwise | flops 524288 | bytes 3145728 | tf_op jit(solution)/shard_map/convert_element_type | solution.py:302
  10.2 0.0 all-gather.2.cloned.1.call-update
  10.2 0.0 copy-done.7
  10.2 0.0 copy-done.4
  10.2 4.2 %shard_map.84.x_ref = f32[2304,128]{1,0:T(8,128)S(1)} custom-call(bf16[256,2048]{1,0:T(8,128)(2,1)S(1)} %copy-done.4, bf16[256,2048]{1,0:T(8,128)(2,1)S(1)} %copy-done.7), custom_call_target="tpu_custom_call" | custom-call | flops 1073741824 | bytes 4194304 | tf_op jit(solution)/shard_map/pallas_call | solution.py:280
  14.4 0.0 copy-start.11
  14.4 61.4 %shard_map.85.e_ref.en_ref = f32[2304,128]{1,0:T(8,128)S(1)} custom-call(f32[2304,128]{1,0:T(8,128)S(1)} %shard_map.84.x_ref), custom_call_target="tpu_custom_call" | custom-call | bytes 100000000 | tf_op jit(solution)/shard_map/pallas_call | solution.py:116
  75.8 0.0 copy-done.11
  75.8 0.0 copy-start
  75.8 0.0 copy-start.2
  75.8 0.0 copy-start.5
  75.8 0.0 copy-start.8
  75.8 6.3 %fusion.da_ref = f32[256,2048]{1,0:T(8,128)S(1)} fusion(bf16[256,2048]{1,0:T(8,128)(2,1)S(1)} %copy-done.11, bf16[2048,2048]{1,0:T(8,128)(2,1)} %param.8), kind=kOutput, calls=%fused_computation | convolution fusion | flops 2147483648 | bytes 11534336 | tf_op jit(solution)/shard_map/dot_general | solution.py:305
  82.1 0.0 copy-done
  82.1 0.0 copy-done.2
  82.1 0.0 copy-done.5
  82.1 0.0 copy-done.8
  82.2 0.0 copy-start.1
  82.2 14.4 %shard_map.86 = (f32[2048,256]{1,0:T(8,128)S(1)}, f32[2304,128]{1,0:T(8,128)S(1)}) custom-call(bf16[256,2048]{1,0:T(8,128)(2,1)S(1)} %copy-done.2, bf16[256,2048]{1,0:T(8,128)(2,1)S(1)} %copy-done.5, bf16[256,2048]{1,0:T(8,128)(2,1)S(1)} %copy-done.8, f32[2304,128]{1,0:T(8,128)S(1)} %shard_map.85.e_ref.en_ref, f32[256,2048]{1,0:T(8,128)S(1)} %fusion.da_ref), custom_call_target="tpu_custom_call" | custom-call | flops 1073741824 | bytes 4194304 | tf_op jit(solution)/shard_map/pallas_call | solution.py:280
  96.6 0.0 copy-done.1
  96.6 0.0 copy-start.9
  96.6 1.3 copy-done.9
  97.9 0.0 copy-start.10
  97.9 1.0 copy-done.10
  98.9 11.4 %all-gather.2.cloned.1.call-done.og_ref = f32[2048,2048]{1,0:T(8,128)} async-done(((f32[256,2048]{1,0:T(8,128)}), f32[2048,2048]{1,0:T(8,128)}) %all-gather.2.cloned.1.call-update) | async-done | bytes 16777232 | tf_op jit(solution)/shard_map/all_gather | solution.py:302
  110.4 0.0 copy-start.3
  110.4 1.2 copy-done.3
  111.6 0.0 copy-start.6
  111.6 1.2 copy-done.6
  112.8 100.6 %shard_map.87 = (bf16[256,2048]{1,0:T(8,128)(2,1)S(1)}, bf16[256,2048]{1,0:T(8,128)(2,1)S(1)}, bf16[256,2048]{1,0:T(8,128)(2,1)S(1)}, f32[64,2048]{1,0:T(8,128)S(1)}) custom-call(f32[2304,128]{1,0:T(8,128)} %copy-done.10, f32[4,8,64,256]{3,2,1,0:T(8,128)} %bitcast.3, f32[2048,2048]{1,0:T(8,128)} %all-gather.2.cloned.1.call-done.og_ref, ...), custom_call_target="tpu_custom_call" | custom-call | bytes 200000000 | tf_op jit(solution)/shard_map/pallas_call | solution.py:204
  213.4 1.0 copy.13
  214.4 1.0 copy.14
  215.4 1.0 copy.15
  216.3 0.8 copy.16
Async XLA Ops:
  7.2 3.0 %copy-start.7 = (bf16[256,2048]{1,0:T(8,128)(2,1)S(1)}, bf16[256,2048]{1,0:T(8,128)(2,1)}, u32[]{:S(2)}) copy-start(bf16[256,2048]{1,0:T(8,128)(2,1)} %v_ref.5) | copy-start | bytes 3145732
  7.2 3.0 %copy-start.4 = (bf16[256,2048]{1,0:T(8,128)(2,1)S(1)}, bf16[256,2048]{1,0:T(8,128)(2,1)}, u32[]{:S(2)}) copy-start(bf16[256,2048]{1,0:T(8,128)(2,1)} %k_ref.5) | copy-start | bytes 3145732
  7.2 103.2 %all-gather.2.cloned.1.call-start = ((), (), s32[]{:S(2)}) async-start(), calls=%async_computation | async-start | bytes 18874368 | tf_op jit(solution)/shard_map/all_gather | solution.py:302
  14.4 61.4 %copy-start.11 = (bf16[256,2048]{1,0:T(8,128)(2,1)S(1)}, bf16[256,2048]{1,0:T(8,128)(2,1)}, u32[]{:S(2)}) copy-start(bf16[256,2048]{1,0:T(8,128)(2,1)} %param.9) | copy-start | bytes 3145732
  75.8 6.3 %copy-start = (f32[2304,128]{1,0:T(8,128)}, f32[2304,128]{1,0:T(8,128)S(1)}, u32[]{:S(2)}) copy-start(f32[2304,128]{1,0:T(8,128)S(1)} %shard_map.85.e_ref.en_ref) | copy-start | bytes 3538948
  75.8 6.3 %copy-start.2 = (bf16[256,2048]{1,0:T(8,128)(2,1)S(1)}, bf16[256,2048]{1,0:T(8,128)(2,1)}, u32[]{:S(2)}) copy-start(bf16[256,2048]{1,0:T(8,128)(2,1)} %q_ref.3) | copy-start | bytes 3145732
  75.8 6.3 %copy-start.5 = (bf16[256,2048]{1,0:T(8,128)(2,1)S(1)}, bf16[256,2048]{1,0:T(8,128)(2,1)}, u32[]{:S(2)}) copy-start(bf16[256,2048]{1,0:T(8,128)(2,1)} %k_ref.5) | copy-start | bytes 3145732
  75.8 6.3 %copy-start.8 = (bf16[256,2048]{1,0:T(8,128)(2,1)S(1)}, bf16[256,2048]{1,0:T(8,128)(2,1)}, u32[]{:S(2)}) copy-start(bf16[256,2048]{1,0:T(8,128)(2,1)} %v_ref.5) | copy-start | bytes 3145732
  82.2 14.4 %copy-start.1 = (f32[256,2048]{1,0:T(8,128)}, f32[256,2048]{1,0:T(8,128)S(1)}, u32[]{:S(2)}) copy-start(f32[256,2048]{1,0:T(8,128)S(1)} %fusion.da_ref) | copy-start | bytes 6291460
  96.6 1.3 copy-start.9
  97.9 1.0 copy-start.10
  110.4 1.2 copy-start.3
  111.6 1.2 copy-start.6
Sparse Core Ops, SparseCore 0:
  10.3 100.0 all-gather.1

commit v4 on v3

--- a/solution.py
+++ b/solution.py
@@ -45,11 +45,10 @@
     return me + (1 - 2 * ((me // (1 << k)) % 2)) * (1 << k)
 
 
-def sweep_up(n, reverse, x_ref, tot, recv, near, su, ru):
+def sweep_up(n, reverse, x_ref, tot, recv, near, su, ru, work):
     me = lax.axis_index("seq")
     rows = x_ref.shape[0]
     base = 0
-    keeps = []
     levels = bits_of(n)
     for k in range(levels):
         half = rows >> (k + 1)
@@ -63,18 +62,28 @@
             send_sem=su.at[k], recv_sem=ru.at[k],
             device_id={"seq": partner_of(me, k)}, device_id_type=MESH)
         copy.start()
+        work()
         copy.wait()
         mine = src[pl.ds(keep, half), :]
         theirs = recv[pl.ds(off, half), :]
         near[pl.ds(off, half), :] = jnp.where(bit == (1 if reverse else 0), mine, theirs)
         if k + 1 < levels:
             tot[pl.ds(keep, half), :] = mine + theirs
-        keeps.append((keep, half, off, bit))
         base = keep
+
+
+def keeps_of(n, rows):
+    me = lax.axis_index("seq")
+    base, keeps = 0, []
+    for k in range(bits_of(n)):
+        half = rows >> (k + 1)
+        bit = (me // (1 << k)) % 2
+        base = pl.multiple_of(base + bit * half, 8)
+        keeps.append((base, half, rows - (rows >> k), bit))
     return keeps
 
 
-def sweep_down(keeps, bits, reverse, e_ref, near, out, sd, rd):
+def sweep_down(keeps, bits, reverse, e_ref, near, out, sd, rd, work):
     me = lax.axis_index("seq")
     if len(keeps) - 1 in bits:
         keep, half, _, _ = keeps[-1]
@@ -91,6 +100,7 @@
             device_id={"seq": partner_of(me, k)}, device_id_type=MESH)
         copy.start()
         e_ref[pl.ds(keep, half), :] = jnp.where(early, now, past)
+        work()
         copy.wait()
 
 
@@ -101,59 +111,108 @@
     pl.semaphore_wait(barrier, len(peers))
 
 
-def scan_kernel(n, x_ref, e_ref, tot, recv, near, out, su, ru, sd, rd):
-    me = lax.axis_index("seq")
-    greet([partner_of(me, k) for k in range(bits_of(n))])
-    keeps = sweep_up(n, False, x_ref, tot, recv, near, su, ru)
-    sweep_down(keeps, range(len(keeps)), False, e_ref, near, out, sd, rd)
+def shares(heads, parts, one):
+    left = iter(range(parts))
+
+    def work():
+        i = next(left)
+        lax.fori_loop(heads * i // parts, heads * (i + 1) // parts, one, 0)
+
+    return work
+
+
+def scan_kernel(n, x_ref, og_ref, w_ref, e_ref, da_ref, tot, recv, near, out, su, ru, sd, rd):
+    levels = bits_of(n)
+    me = lax.axis_index("seq")
+
+    def head(h, carry):
+        at = pl.ds(pl.multiple_of(h * HEAD, HEAD), HEAD)
+        da_ref[:, at] = lax.dot_general(og_ref[...], w_ref[at, :], NT, preferred_element_type=F32)
+        return carry
+
+    work = shares(w_ref.shape[0] // HEAD, 2 * levels, head)
+    greet([partner_of(me, k) for k in range(levels)])
+    sweep_up(n, False, x_ref, tot, recv, near, su, ru, work)
+    sweep_down(keeps_of(n, x_ref.shape[0]), range(levels), False, e_ref, near, out, sd, rd, work)
 
 
 def scan_scratch(n, shape):
     return [pltpu.VMEM(shape, F32)] * 4 + [pltpu.SemaphoreType.DMA((bits_of(n),))] * 4
 
 
-def entering(x, n):
+VM = pl.BlockSpec(memory_space=pltpu.VMEM)
+DMA = pltpu.SemaphoreType.DMA
+
+
+def remote_call(kernel, collective_id, outs, ins, scratch, limit, args):
     return pl.pallas_call(
-        functools.partial(scan_kernel, n),
-        out_shape=jax.ShapeDtypeStruct(x.shape, F32),
-        in_specs=[pl.BlockSpec(memory_space=pltpu.VMEM)],
-        out_specs=pl.BlockSpec(memory_space=pltpu.VMEM),
-        scratch_shapes=scan_scratch(n, x.shape),
+        kernel, out_shape=outs, in_specs=ins, out_specs=[VM] * len(outs), scratch_shapes=scratch,
         compiler_params=pltpu.CompilerParams(
-            collective_id=1, has_side_effects=True, vmem_limit_bytes=24 << 20),
+            collective_id=collective_id, has_side_effects=True, vmem_limit_bytes=limit << 20),
         cost_estimate=pl.CostEstimate(flops=0, bytes_accessed=100_000_000, transcendentals=0),
-    )(x)
-
-
-def grads_kernel(n, plane, x_ref, r_ref, og_ref, q_ref, k_ref, v_ref, en_ref, da_ref,
-                 dq_ref, dk_ref, dv_ref, w_ref, tot, recv, near, out, su, ru, sd, rd,
-                 e_ref, og, rt, part, zr, so, sp, rp, sz, rz):
+    )(*args)
+
+
+def swap_kernel(n, plane, x_ref, r_ref, q_ref, k_ref, v_ref, en_ref, da_ref,
+                rt_ref, near, e_part, dq_ref, dk_ref, dv_ref, tot, recv, out, su, ru, sd, rd, e_ref, sp, rp):
     me = lax.axis_index("seq")
     layers = n // plane
+    levels, low = bits_of(n), bits_of(plane)
     spot, layer = me % plane, me // plane
-    tokens = r_ref.shape[3]
-    load = pltpu.make_async_copy(og_ref, og, so)
-    load.start()
     near_peers = [layer * plane + (spot + j) % plane for j in range(1, plane)]
-    far_peers = [((layer + j) % layers) * plane + spot for j in range(1, layers)]
+    far_peers = [partner_of(me, k) for k in range(low, levels)]
     greet(near_peers + far_peers)
     swaps = []
     for j in range(1, plane):
         copy = pltpu.make_async_remote_copy(
-            src_ref=r_ref.at[:, (spot + j) % plane], dst_ref=rt.at[j],
+            src_ref=r_ref.at[:, (spot + j) % plane], dst_ref=rt_ref.at[j],
             send_sem=sp.at[j], recv_sem=rp.at[j],
             device_id={"seq": near_peers[j - 1]}, device_id_type=MESH)
         copy.start()
         swaps.append(copy)
-    keeps = sweep_up(n, True, x_ref, tot, recv, near, su, ru)
-    rt[0] = r_ref[:, spot]
-    load.wait()
+    heads = q_ref.shape[1] // HEAD
+    pad = x_ref.shape[0] // heads
+
+    def head(h, carry):
+        cols = pl.ds(pl.multiple_of(h * HEAD, HEAD), HEAD)
+        block = pl.ds(pl.multiple_of(h * pad, 8), pad)
+        dq_ref[:, cols], dk_ref[:, cols], dv_ref[:, cols] = local_of(
+            q_ref[:, cols], k_ref[:, cols], v_ref[:, cols], en_ref[block, :], da_ref[:, cols])
+        return carry
+
+    work = shares(heads, 2 * levels - low, head)
+    sweep_up(n, True, x_ref, tot, recv, near, su, ru, work)
+    keeps = keeps_of(n, x_ref.shape[0])
+    sweep_down(keeps, range(low, levels), True, e_ref, near, out, sd, rd, work)
+    e_part[...] = e_ref[pl.ds(keeps[low - 1][0], e_part.shape[0]), :]
+    rt_ref[0] = r_ref[:, spot]
     for copy in swaps:
         copy.wait()
-    step = 512
-
-    def columns(c, carry):
-        cols = pl.ds(pl.multiple_of(c * step, step), step)
+
+
+def sum_out_kernel(n, plane, rt, og_ref, near, e_part, k_ref, v_ref, dkl_ref, dvl_ref,
+                   dk_ref, dv_ref, w_ref, out, sd, rd, e_ref, og, part, zr, so, sz, rz):
+    me = lax.axis_index("seq")
+    layers = n // plane
+    low = bits_of(plane)
+    spot, layer = me % plane, me // plane
+    tokens = rt.shape[3]
+    tiles = so.shape[0]
+    step = og.shape[1] // tiles
+    loads = []
+    for c in range(tiles):
+        at = pl.ds(c * step, step)
+        load = pltpu.make_async_copy(og_ref.at[:, at], og.at[:, at], so.at[c])
+        load.start()
+        loads.append(load)
+    keeps = keeps_of(n, near.shape[0])
+    e_ref[pl.ds(keeps[low - 1][0], e_part.shape[0]), :] = e_part[...]
+    far_peers = [((layer + j) % layers) * plane + spot for j in range(1, layers)]
+    greet(far_peers + [partner_of(me, k) for k in range(low)])
+    sums = []
+    for c in range(tiles):
+        cols = pl.ds(c * step, step)
+        loads[c].wait()
         acc = None
         for j in range(plane):
             rows = pl.ds(pl.multiple_of(((spot - j + plane) % plane) * tokens, tokens), tokens)
@@ -161,28 +220,26 @@
             term = lax.dot_general(left, og[rows, cols].astype(BF), NN, preferred_element_type=F32)
             acc = term if acc is None else acc + term
         part[:, :, cols] = acc.reshape(layers, rt.shape[2], step)
-        return carry
-
-    lax.fori_loop(0, og.shape[1] // step, columns, 0)
-    low = bits_of(plane)
-    sweep_down(keeps, range(low, len(keeps)), True, e_ref, near, out, sd, rd)
-    sums = []
-    for j in range(1, layers):
-        copy = pltpu.make_async_remote_copy(
-            src_ref=part.at[(layer + j) % layers], dst_ref=zr.at[j],
-            send_sem=sz.at[j], recv_sem=rz.at[j],
-            device_id={"seq": far_peers[j - 1]}, device_id_type=MESH)
-        copy.start()
-        sums.append(copy)
-    sweep_down(keeps, range(low), True, e_ref, near, out, sd, rd)
-    heads = q_ref.shape[1] // HEAD
-    pad = x_ref.shape[0] // heads
+        for j in range(1, layers):
+            copy = pltpu.make_async_remote_copy(
+                src_ref=part.at[(layer + j) % layers, :, cols], dst_ref=zr.at[j, :, cols],
+                send_sem=sz.at[c, j], recv_sem=rz.at[c, j],
+                device_id={"seq": far_peers[j - 1]}, device_id_type=MESH)
+            copy.start()
+            sums.append(copy)
+    sweep_down(keeps, range(low), True, e_ref, near, out, sd, rd, lambda: None)
+    heads = k_ref.shape[1] // HEAD
+    pad = near.shape[0] // heads
 
     def head(h, carry):
         cols = pl.ds(pl.multiple_of(h * HEAD, HEAD), HEAD)
         block = pl.ds(pl.multiple_of(h * pad, 8), pad)
-        dq_ref[:, cols], dk_ref[:, cols], dv_ref[:, cols] = gradients_of(
-            q_ref[:, cols], k_ref[:, cols], v_ref[:, cols], en_ref[block, :], da_ref[:, cols], e_ref[block, :])
+        later = e_ref[block, :]
+        fk, kslope = features(k_ref[:, cols])
+        g = split(later[:HEAD, :])
+        dfk = dkl_ref[:, cols] + mm(v_ref[:, cols], g, NN) + later[HEAD:HEAD + 1, :]
+        dk_ref[:, cols] = (dfk * kslope).astype(BF)
+        dv_ref[:, cols] = (dvl_ref[:, cols] + mm(fk, g, NT)).astype(BF)
         return carry
 
     lax.fori_loop(0, heads, head, 0)
@@ -192,29 +249,6 @@
     for j in range(1, layers):
         total = total + zr[j]
     w_ref[...] = total
-
-
-def gradients(x, turned, og, queries, keys, values, entry, attended_grad, n, plane):
-    layers = n // plane
-    rows, tokens = turned.shape
-    width = og.shape[1]
-    mine = rows // n
-    vm = pl.BlockSpec(memory_space=pltpu.VMEM)
-    dma = pltpu.SemaphoreType.DMA
-    return pl.pallas_call(
-        functools.partial(grads_kernel, n, plane),
-        out_shape=[jax.ShapeDtypeStruct(queries.shape, BF)] * 3 + [jax.ShapeDtypeStruct((mine, width), F32)],
-        in_specs=[vm, vm, pl.BlockSpec(memory_space=pl.ANY)] + [vm] * 5,
-        out_specs=[vm] * 4,
-        scratch_shapes=scan_scratch(n, x.shape) + [
-            pltpu.VMEM(x.shape, F32),
-            pltpu.VMEM(og.shape, F32), pltpu.VMEM((plane, layers, mine, tokens), F32),
-            pltpu.VMEM((layers, mine, width), F32), pltpu.VMEM((layers, mine, width), F32),
-            dma, dma((plane,)), dma((plane,)), dma((layers,)), dma((layers,))],
-        compiler_params=pltpu.CompilerParams(
-            collective_id=2, has_side_effects=True, vmem_limit_bytes=48 << 20),
-        cost_estimate=pl.CostEstimate(flops=0, bytes_accessed=200_000_000, transcendentals=0),
-    )(x, turned.reshape(layers, plane, mine, tokens), og, queries, keys, values, entry, attended_grad)
 
 
 def features(x):
@@ -256,18 +290,14 @@
     g_ref[...] = with_row(mm(dn, fq_s, TN), jnp.sum(fq * dden, axis=0, keepdims=True), g_ref.shape[0])
 
 
-def gradients_of(q, k, v, entry, da, later):
+def local_of(q, k, v, entry, da):
     fq, fq_s, qslope, fk_s, causal, scores, z, inv, att = forward_of(q, k, v, entry)
-    kslope = jnp.where(k.astype(F32) > 0, 1.0, jnp.exp(jnp.minimum(k.astype(F32), 0.0)))
     dn = da * inv
     dden = -jnp.sum(dn * att, axis=1, keepdims=True)
     dn_s = split(dn)
     dp = split(jnp.where(causal, mm(dn_s, v, NT) + dden, 0.0))
-    g = split(later[:HEAD, :])
     dfq = mm(dp, fk_s, NN) + mm(dn_s, entry[:HEAD, :], NN) + dden * z
-    dfk = mm(dp, fq_s, TN) + mm(v, g, NN) + later[HEAD:HEAD + 1, :]
-    dv = mm(scores, dn_s, TN) + mm(fk_s, g, NT)
-    return (dfq * qslope).astype(BF), (dfk * kslope).astype(BF), dv.astype(BF)
+    return (dfq * qslope).astype(BF), mm(dp, fq_s, TN), mm(scores, dn_s, TN)
 
 
 def per_head(kernel, heads, tokens, pad, ins, outs, args):
@@ -301,13 +331,33 @@
     blocks = [list(range(at, at + plane)) for at in range(0, n, plane)]
     gathered = lax.all_gather(out_grad.astype(F32), "seq", axis_index_groups=blocks, tiled=True)
     (part,) = run(sum_kernel, ins="tt", outs=[("s", F32)], args=(keys, values))
-    entry = entering(part, n)
-    attended_grad = lax.dot_general(out_grad, out_weight, NT, preferred_element_type=F32)
+    layers, low, levels = n // plane, bits_of(plane), bits_of(n)
+    like = jax.ShapeDtypeStruct
+    state, acts = part.shape, queries.shape
+    mine, out_width = width // n, out_grad.shape[1]
+    entry, attended_grad = remote_call(
+        functools.partial(scan_kernel, n), 1, [like(state, F32), like(acts, F32)], [VM] * 3,
+        scan_scratch(n, state), 32, (part, out_grad, out_weight))
     turned, part_grad = run(
         attend_kernel, ins="tttst", outs=[("r", F32), ("s", F32)],
         args=(queries, keys, values, entry, attended_grad))
-    query_grad, key_grad, value_grad, weight_grad = gradients(
-        part_grad, turned, gathered, queries, keys, values, entry, attended_grad, n, plane)
+    swap = (plane, layers, mine, tokens)
+    rt, near, e_part, query_grad, key_part, value_part = remote_call(
+        functools.partial(swap_kernel, n, plane), 2,
+        [like(swap, F32), like(state, F32), like((state[0] >> low, HEAD), F32),
+         like(acts, BF), like(acts, F32), like(acts, F32)],
+        [VM] * 7,
+        [pltpu.VMEM(state, F32)] * 3 + [DMA((levels,))] * 4 + [pltpu.VMEM(state, F32)] + [DMA((plane,))] * 2, 40,
+        (part_grad, turned.reshape(layers, plane, mine, tokens), queries, keys, values, entry, attended_grad))
+    tiles = 4
+    key_grad, value_grad, weight_grad = remote_call(
+        functools.partial(sum_out_kernel, n, plane), 3,
+        [like(acts, BF), like(acts, BF), like((mine, out_width), F32)],
+        [VM, pl.BlockSpec(memory_space=pl.ANY)] + [VM] * 6,
+        [pltpu.VMEM(state, F32)] + [DMA((low,))] * 2 + [pltpu.VMEM(state, F32), pltpu.VMEM(gathered.shape, F32)]
+        + [pltpu.VMEM((layers, mine, out_width), F32)] * 2
+        + [DMA((tiles,))] + [DMA((tiles, layers))] * 2, 46,
+        (rt, gathered, near, e_part, keys, values, key_part, value_part))
     return (query_grad, key_grad, value_grad, weight_grad)
 
 

time: 224 us -> 230 us (1.027)
  Pallas kernels: 181 us -> 198 us
  waiting for transfers between devices: 11.4 us -> 0.02 us
  local copies, waits for them, and re-layouts: 8.54 us -> 15 us
  matrix products: 6.28 us -> 0 us
    pallas_call x2 -> x3, Pallas kernels: 162 us -> 179 us  [remote_call(): pl.pallas_call(kernel, out_shape=outs, in_specs=ins, out_specs=[VM] * len...]
    all_gather x1, waiting for transfers between devices: 11.4 us -> 0.01 us  [body(): lax.all_gather(out_grad.astype(F32), 'seq', axis_index_groups=blocks, til...]
    unnamed x28 -> x30, local copies, waits for them, and re-layouts: 8.54 us -> 15 us
    dot_general x1 -> x0, matrix products: 6.28 us -> none  [body(): lax.dot_general(out_grad, out_weight, NT, preferred_element_type=F32)]
  transfers between devices with their start and end apart: 1 -> 1, of which waited for: 1 -> 0; matrix products, arithmetic and copies ran while one was open for 3% -> 0% of each run, Pallas kernels for 36% -> 64%
where the time goes in v4:
time: 230 us
  Pallas kernels  198 us (86%)
  local copies, waits for them, and re-layouts  15 us (7%)
  between operations  14.2 us (6%)
  other arithmetic  2.95 us (1%)
    pallas_call x3, Pallas kernels, remote_call(): pl.pallas_call(kernel, out_shape=outs, in_specs=ins, out_specs=[VM] * len...  179 us
    pallas_call x2, Pallas kernels, per_head(): pl.pallas_call(kernel, grid=(heads,), in_specs=[spec[i] for i in ins], ou...  18.6 us
    unnamed x30, local copies, waits for them, and re-layouts  15 us
  transfers between devices with their start and end apart: 1, of which 0 were waited for; matrix products, arithmetic and copies ran while one was open for 0% of the time, Pallas kernels for 64%

profile of v4, /device:TPU:0, one launch (start us, length us, event | category | flops | bytes accessed | tf_op | source)
XLA Modules:
  0.0 229.9 jit_solution(16157004364417316147)
XLA Ops:
  7.2 0.0 copy-start
  7.2 0.0 copy-start.1
  7.2 0.0 all-gather.2.cloned.1.call-start
  7.2 2.9 %convert_element_type.3 = f32[256,2048]{1,0:T(8,128)} convert(bf16[256,2048]{1,0:T(8,128)(2,1)} %og_ref.1) | non-fusion elementwise | flops 524288 | bytes 3145728 | tf_op jit(solution)/shard_map/convert_element_type | solution.py:332
  10.2 0.0 all-gather.2.cloned.1.call-update
  10.2 0.0 copy-done
  10.2 0.0 copy-done.1
  10.2 0.0 copy-start.5
  10.2 4.2 %shard_map.84.x_ref = f32[2304,128]{1,0:T(8,128)S(1)} custom-call(bf16[256,2048]{1,0:T(8,128)(2,1)S(1)} %copy-done, bf16[256,2048]{1,0:T(8,128)(2,1)S(1)} %copy-done.1), custom_call_target="tpu_custom_call" | custom-call | flops 1073741824 | bytes 4194304 | tf_op jit(solution)/shard_map/pallas_call | solution.py:310
  14.4 0.0 copy-done.5
  14.4 0.0 copy-start.3
  14.4 3.4 %copy-done.3 = bf16[2048,2048]{1,0:T(8,128)(2,1)S(1)} copy-done((bf16[2048,2048]{1,0:T(8,128)(2,1)S(1)}, bf16[2048,2048]{1,0:T(8,128)(2,1)}, u32[]{:S(2)}) %copy-start.3) | copy-done | bytes 8388632
  17.8 0.0 copy-start.4
  17.8 64.7 %shard_map.85 = (f32[2304,128]{1,0:T(8,128)S(1)}, f32[256,2048]{1,0:T(8,128)S(1)}) custom-call(f32[2304,128]{1,0:T(8,128)S(1)} %shard_map.84.x_ref, bf16[256,2048]{1,0:T(8,128)(2,1)S(1)} %copy-done.5, bf16[2048,2048]{1,0:T(8,128)(2,1)S(1)} %copy-done.3), custom_call_target="tpu_custom_call" | custom-call | bytes 100000000 | tf_op jit(solution)/shard_map/pallas_call | solution.py:148
  82.6 0.0 copy-start.2
  82.6 0.0 copy-done.4
  82.6 14.4 %shard_map.86 = (f32[2048,256]{1,0:T(8,128)S(1)}, f32[2304,128]{1,0:T(8,128)S(1)}) custom-call(bf16[256,2048]{1,0:T(8,128)(2,1)S(1)} %copy-done.4, bf16[256,2048]{1,0:T(8,128)(2,1)S(1)} %copy-done, bf16[256,2048]{1,0:T(8,128)(2,1)S(1)} %copy-done.1, f32[2304,128]{1,0:T(8,128)S(1)} %get-tuple-element.17.e_ref.en_ref, f32[256,2048]{1,0:T(8,128)S(1)} %get-tuple-element.18.da_ref), custom_call_target="tpu_custom_call" | custom-call | flops 1073741824 | bytes 4194304 | tf_op jit(solution)/shard_map/pallas_call | solution.py:310
  97.0 0.0 copy-done.2
  97.0 0.0 copy-start.10
  97.0 1.3 copy-done.10
  98.3 63.7 %shard_map.87 = (f32[8,4,64,256]{3,2,1,0:T(8,128)S(1)}, f32[2304,128]{1,0:T(8,128)S(1)}, f32[288,128]{1,0:T(8,128)S(1)}, bf16[256,2048]{1,0:T(8,128)(2,1)S(1)}, ...) custom-call(f32[2304,128]{1,0:T(8,128)S(1)} %get-tuple-element.19.x_ref, f32[4,8,64,256]{3,2,1,0:T(8,128)} %bitcast.1, ...), custom_call_target="tpu_custom_call" | custom-call | bytes 100000000 | tf_op jit(solution)/shard_map/pallas_call | solution.py:148
  162.0 0.0 copy-start.6
  162.0 1.3 copy-done.6
  163.3 0.0 copy-start.8
  163.3 1.3 copy-done.8
  164.7 0.0 copy-start.9
  164.7 1.4 copy-done.9
  166.0 0.0 copy-start.11
  166.0 1.0 copy-done.11
  167.0 0.0 all-gather.2.cloned.1.call-done.og_ref
  167.0 0.0 copy-start.7
  167.0 1.6 copy-done.7
  168.6 0.0 copy-start.12
  168.6 50.7 %shard_map.88 = (bf16[256,2048]{1,0:T(8,128)(2,1)S(1)}, bf16[256,2048]{1,0:T(8,128)(2,1)S(1)}, f32[64,2048]{1,0:T(8,128)S(1)}) custom-call(f32[8,4,64,256]{3,2,1,0:T(8,128)S(1)} %copy-done.7, f32[2048,2048]{1,0:T(8,128)} %all-gather.2.cloned.1.call-done.og_ref, f32[2304,128]{1,0:T(8,128)S(1)} %get-tuple-element.23.near, ...), custom_call_target="tpu_custom_call" | custom-call | bytes 100000000 | tf_op jit(solution)/shard_map/pallas_call | solution.py:148
  219.3 0.0 copy-done.12
  219.4 1.0 copy.13
  220.3 1.0 copy.14
  221.3 1.0 copy.15
  222.3 0.8 copy.16
Async XLA Ops:
  7.2 3.0 %copy-start = (bf16[256,2048]{1,0:T(8,128)(2,1)S(1)}, bf16[256,2048]{1,0:T(8,128)(2,1)}, u32[]{:S(2)}) copy-start(bf16[256,2048]{1,0:T(8,128)(2,1)} %k_ref.7) | copy-start | bytes 3145732
  7.2 3.0 %copy-start.1 = (bf16[256,2048]{1,0:T(8,128)(2,1)S(1)}, bf16[256,2048]{1,0:T(8,128)(2,1)}, u32[]{:S(2)}) copy-start(bf16[256,2048]{1,0:T(8,128)(2,1)} %v_ref.7) | copy-start | bytes 3145732
  7.2 159.8 %all-gather.2.cloned.1.call-start = ((), (), s32[]{:S(2)}) async-start(), calls=%async_computation | async-start | bytes 18874368 | tf_op jit(solution)/shard_map/all_gather | solution.py:332
  10.2 4.2 %copy-start.5 = (bf16[256,2048]{1,0:T(8,128)(2,1)S(1)}, bf16[256,2048]{1,0:T(8,128)(2,1)}, u32[]{:S(2)}) copy-start(bf16[256,2048]{1,0:T(8,128)(2,1)} %og_ref.1) | copy-start | bytes 3145732
  14.4 3.4 %copy-start.3 = (bf16[2048,2048]{1,0:T(8,128)(2,1)S(1)}, bf16[2048,2048]{1,0:T(8,128)(2,1)}, u32[]{:S(2)}) copy-start(bf16[2048,2048]{1,0:T(8,128)(2,1)} %w_ref.1) | copy-start | bytes 25165828
  17.8 64.8 %copy-start.4 = (bf16[256,2048]{1,0:T(8,128)(2,1)S(1)}, bf16[256,2048]{1,0:T(8,128)(2,1)}, u32[]{:S(2)}) copy-start(bf16[256,2048]{1,0:T(8,128)(2,1)} %q_ref.3) | copy-start | bytes 3145732
  82.6 14.4 %copy-start.2 = (f32[256,2048]{1,0:T(8,128)}, f32[256,2048]{1,0:T(8,128)S(1)}, u32[]{:S(2)}) copy-start(f32[256,2048]{1,0:T(8,128)S(1)} %get-tuple-element.18.da_ref) | copy-start | bytes 6291460
  97.0 1.3 copy-start.10
  162.0 1.4 copy-start.6
  163.3 1.3 copy-start.8
  164.7 1.4 copy-start.9
  166.0 1.0 copy-start.11
  167.0 1.6 copy-start.7
  168.6 50.8 %copy-start.12 = (bf16[256,2048]{1,0:T(8,128)(2,1)S(1)}, bf16[256,2048]{1,0:T(8,128)(2,1)}, u32[]{:S(2)}) copy-start(bf16[256,2048]{1,0:T(8,128)(2,1)} %copy-done.11) | copy-start | bytes 3145732
Sparse Core Ops, SparseCore 0:
  10.3 111.2 all-gather.1

commit v5 on v4

--- a/solution.py
+++ b/solution.py
@@ -164,12 +164,10 @@
     greet(near_peers + far_peers)
     swaps = []
     for j in range(1, plane):
-        copy = pltpu.make_async_remote_copy(
+        swaps.append(pltpu.make_async_remote_copy(
             src_ref=r_ref.at[:, (spot + j) % plane], dst_ref=rt_ref.at[j],
             send_sem=sp.at[j], recv_sem=rp.at[j],
-            device_id={"seq": near_peers[j - 1]}, device_id_type=MESH)
-        copy.start()
-        swaps.append(copy)
+            device_id={"seq": near_peers[j - 1]}, device_id_type=MESH))
     heads = q_ref.shape[1] // HEAD
     pad = x_ref.shape[0] // heads
 
@@ -180,7 +178,15 @@
             q_ref[:, cols], k_ref[:, cols], v_ref[:, cols], en_ref[block, :], da_ref[:, cols])
         return carry
 
-    work = shares(heads, 2 * levels - low, head)
+    turns = iter(range(2 * levels))
+    share = shares(heads, 2 * levels - low, head)
+
+    def work():
+        if next(turns) == low:
+            for copy in swaps:
+                copy.start()
+        share()
+
     sweep_up(n, True, x_ref, tot, recv, near, su, ru, work)
     keeps = keeps_of(n, x_ref.shape[0])
     sweep_down(keeps, range(low, levels), True, e_ref, near, out, sd, rd, work)
@@ -337,7 +343,7 @@
     mine, out_width = width // n, out_grad.shape[1]
     entry, attended_grad = remote_call(
         functools.partial(scan_kernel, n), 1, [like(state, F32), like(acts, F32)], [VM] * 3,
-        scan_scratch(n, state), 32, (part, out_grad, out_weight))
+        scan_scratch(n, state), 12, (part, out_grad, out_weight))
     turned, part_grad = run(
         attend_kernel, ins="tttst", outs=[("r", F32), ("s", F32)],
         args=(queries, keys, values, entry, attended_grad))
@@ -347,7 +353,7 @@
         [like(swap, F32), like(state, F32), like((state[0] >> low, HEAD), F32),
          like(acts, BF), like(acts, F32), like(acts, F32)],
         [VM] * 7,
-        [pltpu.VMEM(state, F32)] * 3 + [DMA((levels,))] * 4 + [pltpu.VMEM(state, F32)] + [DMA((plane,))] * 2, 40,
+        [pltpu.VMEM(state, F32)] * 3 + [DMA((levels,))] * 4 + [pltpu.VMEM(state, F32)] + [DMA((plane,))] * 2, 12,
         (part_grad, turned.reshape(layers, plane, mine, tokens), queries, keys, values, entry, attended_grad))
     tiles = 4
     key_grad, value_grad, weight_grad = remote_call(
@@ -356,7 +362,7 @@
         [VM, pl.BlockSpec(memory_space=pl.ANY)] + [VM] * 6,
         [pltpu.VMEM(state, F32)] + [DMA((low,))] * 2 + [pltpu.VMEM(state, F32), pltpu.VMEM(gathered.shape, F32)]
         + [pltpu.VMEM((layers, mine, out_width), F32)] * 2
-        + [DMA((tiles,))] + [DMA((tiles, layers))] * 2, 46,
+        + [DMA((tiles,))] + [DMA((tiles, layers))] * 2, 28,
         (rt, gathered, near, e_part, keys, values, key_part, value_part))
     return (query_grad, key_grad, value_grad, weight_grad)
 

time: 230 us -> 216 us (0.939)
  Pallas kernels: 198 us -> 182 us
    pallas_call x3, Pallas kernels: 179 us -> 164 us  [remote_call(): pl.pallas_call(kernel, out_shape=outs, in_specs=ins, out_specs=[VM] * len...]
  transfers between devices with their start and end apart: 1 -> 1, of which waited for: 0 -> 0; matrix products, arithmetic and copies ran while one was open for 0% -> 0% of each run, Pallas kernels for 64% -> 62%
where the time goes in v5:
time: 216 us
  Pallas kernels  182 us (84%)
  local copies, waits for them, and re-layouts  16.9 us (8%)
  between operations  14.2 us (7%)
  other arithmetic  2.95 us (1%)
    pallas_call x3, Pallas kernels, remote_call(): pl.pallas_call(kernel, out_shape=outs, in_specs=ins, out_specs=[VM] * len...  164 us
    pallas_call x2, Pallas kernels, per_head(): pl.pallas_call(kernel, grid=(heads,), in_specs=[spec[i] for i in ins], ou...  18.6 us
    unnamed x30, local copies, waits for them, and re-layouts  16.9 us
  transfers between devices with their start and end apart: 1, of which 0 were waited for; matrix products, arithmetic and copies ran while one was open for 0% of the time, Pallas kernels for 62%

profile of v5, /device:TPU:0, one launch (start us, length us, event | category | flops | bytes accessed | tf_op | source)
XLA Modules:
  0.0 216.2 jit_solution(16204772823081326398)
XLA Ops:
  7.2 0.0 copy-start
  7.2 0.0 copy-start.1
  7.2 0.0 all-gather.2.cloned.1.call-start
  7.2 2.9 %convert_element_type.3 = f32[256,2048]{1,0:T(8,128)} convert(bf16[256,2048]{1,0:T(8,128)(2,1)} %og_ref.1) | non-fusion elementwise | flops 524288 | bytes 3145728 | tf_op jit(solution)/shard_map/convert_element_type | solution.py:338
  10.2 0.0 all-gather.2.cloned.1.call-update
  10.2 0.0 copy-done
  10.2 0.0 copy-done.1
  10.2 0.0 copy-start.4
  10.2 4.2 %shard_map.84.x_ref = f32[2304,128]{1,0:T(8,128)S(1)} custom-call(bf16[256,2048]{1,0:T(8,128)(2,1)S(1)} %copy-done, bf16[256,2048]{1,0:T(8,128)(2,1)S(1)} %copy-done.1), custom_call_target="tpu_custom_call" | custom-call | flops 1073741824 | bytes 4194304 | tf_op jit(solution)/shard_map/pallas_call | solution.py:316
  14.4 0.0 copy-done.4
  14.4 0.0 copy-start.2
  14.4 3.4 %copy-done.2 = bf16[2048,2048]{1,0:T(8,128)(2,1)S(1)} copy-done((bf16[2048,2048]{1,0:T(8,128)(2,1)S(1)}, bf16[2048,2048]{1,0:T(8,128)(2,1)}, u32[]{:S(2)}) %copy-start.2) | copy-done | bytes 8388632
  17.8 0.0 copy-start.3
  17.8 64.7 %shard_map.85 = (f32[2304,128]{1,0:T(8,128)S(1)}, f32[256,2048]{1,0:T(8,128)S(1)}) custom-call(f32[2304,128]{1,0:T(8,128)S(1)} %shard_map.84.x_ref, bf16[256,2048]{1,0:T(8,128)(2,1)S(1)} %copy-done.4, bf16[2048,2048]{1,0:T(8,128)(2,1)S(1)} %copy-done.2), custom_call_target="tpu_custom_call" | custom-call | bytes 100000000 | tf_op jit(solution)/shard_map/pallas_call | solution.py:148
  82.6 0.0 copy-done.3
  82.6 14.4 %shard_map.86 = (f32[2048,256]{1,0:T(8,128)S(1)}, f32[2304,128]{1,0:T(8,128)S(1)}) custom-call(bf16[256,2048]{1,0:T(8,128)(2,1)S(1)} %copy-done.3, bf16[256,2048]{1,0:T(8,128)(2,1)S(1)} %copy-done, bf16[256,2048]{1,0:T(8,128)(2,1)S(1)} %copy-done.1, f32[2304,128]{1,0:T(8,128)S(1)} %get-tuple-element.17.e_ref.en_ref, f32[256,2048]{1,0:T(8,128)S(1)} %get-tuple-element.18.da_ref), custom_call_target="tpu_custom_call" | custom-call | flops 1073741824 | bytes 4194304 | tf_op jit(solution)/shard_map/pallas_call | solution.py:316
  97.0 50.4 %shard_map.87 = (f32[8,4,64,256]{3,2,1,0:T(8,128)S(1)}, f32[2304,128]{1,0:T(8,128)S(1)}, f32[288,128]{1,0:T(8,128)S(1)}, bf16[256,2048]{1,0:T(8,128)(2,1)S(1)}, ...) custom-call(f32[2304,128]{1,0:T(8,128)S(1)} %get-tuple-element.19.x_ref, f32[4,8,64,256]{3,2,1,0:T(8,128)S(1)} %bitcast.1, ...), custom_call_target="tpu_custom_call" | custom-call | bytes 100000000 | tf_op jit(solution)/shard_map/pallas_call | solution.py:148
  147.4 0.0 copy-start.5
  147.4 1.3 copy-done.5
  148.7 0.0 copy-start.7
  148.7 1.4 copy-done.7
  150.0 0.0 copy-start.9
  150.0 1.4 copy-done.9
  151.4 0.0 copy-start.11
  151.4 1.0 copy-done.11
  152.4 0.0 all-gather.2.cloned.1.call-done.og_ref
  152.4 0.0 copy-start.6
  152.4 1.6 copy-done.6
  154.0 0.0 copy-start.8
  154.0 1.6 copy-done.8
  155.5 0.0 copy-start.10
  155.6 1.6 copy-done.10
  157.1 0.0 copy-start.12
  157.1 48.5 %shard_map.88 = (bf16[256,2048]{1,0:T(8,128)(2,1)S(1)}, bf16[256,2048]{1,0:T(8,128)(2,1)S(1)}, f32[64,2048]{1,0:T(8,128)S(1)}) custom-call(f32[8,4,64,256]{3,2,1,0:T(8,128)S(1)} %copy-done.6, f32[2048,2048]{1,0:T(8,128)} %all-gather.2.cloned.1.call-done.og_ref, f32[2304,128]{1,0:T(8,128)S(1)} %get-tuple-element.23.near, ...), custom_call_target="tpu_custom_call" | custom-call | bytes 100000000 | tf_op jit(solution)/shard_map/pallas_call | solution.py:148
  205.6 0.0 copy-done.12
  205.7 1.0 copy.13
  206.6 1.0 copy.14
  207.6 1.0 copy.15
  208.6 0.8 copy.16
Async XLA Ops:
  7.2 3.0 %copy-start = (bf16[256,2048]{1,0:T(8,128)(2,1)S(1)}, bf16[256,2048]{1,0:T(8,128)(2,1)}, u32[]{:S(2)}) copy-start(bf16[256,2048]{1,0:T(8,128)(2,1)} %k_ref.7) | copy-start | bytes 3145732
  7.2 3.0 %copy-start.1 = (bf16[256,2048]{1,0:T(8,128)(2,1)S(1)}, bf16[256,2048]{1,0:T(8,128)(2,1)}, u32[]{:S(2)}) copy-start(bf16[256,2048]{1,0:T(8,128)(2,1)} %v_ref.7) | copy-start | bytes 3145732
  7.2 145.2 %all-gather.2.cloned.1.call-start = ((), (), s32[]{:S(2)}) async-start(), calls=%async_computation | async-start | bytes 18874368 | tf_op jit(solution)/shard_map/all_gather | solution.py:338
  10.2 4.2 %copy-start.4 = (bf16[256,2048]{1,0:T(8,128)(2,1)S(1)}, bf16[256,2048]{1,0:T(8,128)(2,1)}, u32[]{:S(2)}) copy-start(bf16[256,2048]{1,0:T(8,128)(2,1)} %og_ref.1) | copy-start | bytes 3145732
  14.4 3.4 %copy-start.2 = (bf16[2048,2048]{1,0:T(8,128)(2,1)S(1)}, bf16[2048,2048]{1,0:T(8,128)(2,1)}, u32[]{:S(2)}) copy-start(bf16[2048,2048]{1,0:T(8,128)(2,1)} %w_ref.1) | copy-start | bytes 25165828
  17.8 64.8 %copy-start.3 = (bf16[256,2048]{1,0:T(8,128)(2,1)S(1)}, bf16[256,2048]{1,0:T(8,128)(2,1)}, u32[]{:S(2)}) copy-start(bf16[256,2048]{1,0:T(8,128)(2,1)} %q_ref.3) | copy-start | bytes 3145732
  147.4 1.3 copy-start.5
  148.7 1.4 copy-start.7
  150.0 1.4 copy-start.9
  151.4 1.0 copy-start.11
  152.4 1.6 copy-start.6
  154.0 1.6 copy-start.8
  155.5 1.6 copy-start.10
  157.1 48.5 %copy-start.12 = (bf16[256,2048]{1,0:T(8,128)(2,1)S(1)}, bf16[256,2048]{1,0:T(8,128)(2,1)}, u32[]{:S(2)}) copy-start(bf16[256,2048]{1,0:T(8,128)(2,1)} %copy-done.11) | copy-start | bytes 3145732
Sparse Core Ops, SparseCore 0:
  10.3 110.3 all-gather.1

commit v6 on v5

--- a/solution.py
+++ b/solution.py
@@ -182,7 +182,7 @@
     share = shares(heads, 2 * levels - low, head)
 
     def work():
-        if next(turns) == low:
+        if next(turns) == low - 1:
             for copy in swaps:
                 copy.start()
         share()

time: 216 us -> 218 us (level)
  no operation moved by 1% of the time
where the time goes in v6:
time: 218 us
  Pallas kernels  184 us (84%)
  local copies, waits for them, and re-layouts  16.9 us (8%)
  between operations  14.2 us (7%)
  other arithmetic  2.95 us (1%)
    pallas_call x3, Pallas kernels, remote_call(): pl.pallas_call(kernel, out_shape=outs, in_specs=ins, out_specs=[VM] * len...  165 us
    pallas_call x2, Pallas kernels, per_head(): pl.pallas_call(kernel, grid=(heads,), in_specs=[spec[i] for i in ins], ou...  18.6 us
    unnamed x30, local copies, waits for them, and re-layouts  16.9 us
  transfers between devices with their start and end apart: 1, of which 0 were waited for; matrix products, arithmetic and copies ran while one was open for 0% of the time, Pallas kernels for 62%

profile of v6, /device:TPU:0, one launch (start us, length us, event | category | flops | bytes accessed | tf_op | source)
XLA Modules:
  0.0 217.6 jit_solution(1361230753685203405)
XLA Ops:
  7.2 0.0 copy-start
  7.2 0.0 copy-start.1
  7.2 0.0 all-gather.2.cloned.1.call-start
  7.2 2.9 %convert_element_type.3 = f32[256,2048]{1,0:T(8,128)} convert(bf16[256,2048]{1,0:T(8,128)(2,1)} %og_ref.1) | non-fusion elementwise | flops 524288 | bytes 3145728 | tf_op jit(solution)/shard_map/convert_element_type | solution.py:338
  10.2 0.0 all-gather.2.cloned.1.call-update
  10.2 0.0 copy-done
  10.2 0.0 copy-done.1
  10.2 0.0 copy-start.4
  10.2 4.2 %shard_map.84.x_ref = f32[2304,128]{1,0:T(8,128)S(1)} custom-call(bf16[256,2048]{1,0:T(8,128)(2,1)S(1)} %copy-done, bf16[256,2048]{1,0:T(8,128)(2,1)S(1)} %copy-done.1), custom_call_target="tpu_custom_call" | custom-call | flops 1073741824 | bytes 4194304 | tf_op jit(solution)/shard_map/pallas_call | solution.py:316
  14.4 0.0 copy-done.4
  14.4 0.0 copy-start.2
  14.4 3.4 %copy-done.2 = bf16[2048,2048]{1,0:T(8,128)(2,1)S(1)} copy-done((bf16[2048,2048]{1,0:T(8,128)(2,1)S(1)}, bf16[2048,2048]{1,0:T(8,128)(2,1)}, u32[]{:S(2)}) %copy-start.2) | copy-done | bytes 8388632
  17.8 0.0 copy-start.3
  17.8 64.7 %shard_map.85 = (f32[2304,128]{1,0:T(8,128)S(1)}, f32[256,2048]{1,0:T(8,128)S(1)}) custom-call(f32[2304,128]{1,0:T(8,128)S(1)} %shard_map.84.x_ref, bf16[256,2048]{1,0:T(8,128)(2,1)S(1)} %copy-done.4, bf16[2048,2048]{1,0:T(8,128)(2,1)S(1)} %copy-done.2), custom_call_target="tpu_custom_call" | custom-call | bytes 100000000 | tf_op jit(solution)/shard_map/pallas_call | solution.py:148
  82.6 0.0 copy-done.3
  82.6 14.4 %shard_map.86 = (f32[2048,256]{1,0:T(8,128)S(1)}, f32[2304,128]{1,0:T(8,128)S(1)}) custom-call(bf16[256,2048]{1,0:T(8,128)(2,1)S(1)} %copy-done.3, bf16[256,2048]{1,0:T(8,128)(2,1)S(1)} %copy-done, bf16[256,2048]{1,0:T(8,128)(2,1)S(1)} %copy-done.1, f32[2304,128]{1,0:T(8,128)S(1)} %get-tuple-element.17.e_ref.en_ref, f32[256,2048]{1,0:T(8,128)S(1)} %get-tuple-element.18.da_ref), custom_call_target="tpu_custom_call" | custom-call | flops 1073741824 | bytes 4194304 | tf_op jit(solution)/shard_map/pallas_call | solution.py:316
  97.0 52.7 %shard_map.87 = (f32[8,4,64,256]{3,2,1,0:T(8,128)S(1)}, f32[2304,128]{1,0:T(8,128)S(1)}, f32[288,128]{1,0:T(8,128)S(1)}, bf16[256,2048]{1,0:T(8,128)(2,1)S(1)}, ...) custom-call(f32[2304,128]{1,0:T(8,128)S(1)} %get-tuple-element.19.x_ref, f32[4,8,64,256]{3,2,1,0:T(8,128)S(1)} %bitcast.1, ...), custom_call_target="tpu_custom_call" | custom-call | bytes 100000000 | tf_op jit(solution)/shard_map/pallas_call | solution.py:148
  149.7 0.0 copy-start.5
  149.7 1.3 copy-done.5
  151.0 0.0 copy-start.7
  151.0 1.4 copy-done.7
  152.4 0.0 copy-start.9
  152.4 1.4 copy-done.9
  153.7 0.0 copy-start.11
  153.7 1.0 copy-done.11
  154.7 0.0 all-gather.2.cloned.1.call-done.og_ref
  154.7 0.0 copy-start.6
  154.7 1.6 copy-done.6
  156.3 0.0 copy-start.8
  156.3 1.6 copy-done.8
  157.9 0.0 copy-start.10
  157.9 1.6 copy-done.10
  159.5 0.0 copy-start.12
  159.5 47.5 %shard_map.88 = (bf16[256,2048]{1,0:T(8,128)(2,1)S(1)}, bf16[256,2048]{1,0:T(8,128)(2,1)S(1)}, f32[64,2048]{1,0:T(8,128)S(1)}) custom-call(f32[8,4,64,256]{3,2,1,0:T(8,128)S(1)} %copy-done.6, f32[2048,2048]{1,0:T(8,128)} %all-gather.2.cloned.1.call-done.og_ref, f32[2304,128]{1,0:T(8,128)S(1)} %get-tuple-element.23.near, ...), custom_call_target="tpu_custom_call" | custom-call | bytes 100000000 | tf_op jit(solution)/shard_map/pallas_call | solution.py:148
  207.0 0.0 copy-done.12
  207.0 1.0 copy.13
  208.0 1.0 copy.14
  209.0 1.0 copy.15
  209.9 0.8 copy.16
Async XLA Ops:
  7.2 3.0 %copy-start = (bf16[256,2048]{1,0:T(8,128)(2,1)S(1)}, bf16[256,2048]{1,0:T(8,128)(2,1)}, u32[]{:S(2)}) copy-start(bf16[256,2048]{1,0:T(8,128)(2,1)} %k_ref.7) | copy-start | bytes 3145732
  7.2 3.0 %copy-start.1 = (bf16[256,2048]{1,0:T(8,128)(2,1)S(1)}, bf16[256,2048]{1,0:T(8,128)(2,1)}, u32[]{:S(2)}) copy-start(bf16[256,2048]{1,0:T(8,128)(2,1)} %v_ref.7) | copy-start | bytes 3145732
  7.2 147.5 %all-gather.2.cloned.1.call-start = ((), (), s32[]{:S(2)}) async-start(), calls=%async_computation | async-start | bytes 18874368 | tf_op jit(solution)/shard_map/all_gather | solution.py:338
  10.2 4.2 %copy-start.4 = (bf16[256,2048]{1,0:T(8,128)(2,1)S(1)}, bf16[256,2048]{1,0:T(8,128)(2,1)}, u32[]{:S(2)}) copy-start(bf16[256,2048]{1,0:T(8,128)(2,1)} %og_ref.1) | copy-start | bytes 3145732
  14.4 3.4 %copy-start.2 = (bf16[2048,2048]{1,0:T(8,128)(2,1)S(1)}, bf16[2048,2048]{1,0:T(8,128)(2,1)}, u32[]{:S(2)}) copy-start(bf16[2048,2048]{1,0:T(8,128)(2,1)} %w_ref.1) | copy-start | bytes 25165828
  17.8 64.8 %copy-start.3 = (bf16[256,2048]{1,0:T(8,128)(2,1)S(1)}, bf16[256,2048]{1,0:T(8,128)(2,1)}, u32[]{:S(2)}) copy-start(bf16[256,2048]{1,0:T(8,128)(2,1)} %q_ref.3) | copy-start | bytes 3145732
  149.7 1.3 copy-start.5
  151.0 1.4 copy-start.7
  152.4 1.4 copy-start.9
  153.7 1.0 copy-start.11
  154.7 1.6 copy-start.6
  156.3 1.6 copy-start.8
  157.9 1.6 copy-start.10
  159.5 47.6 %copy-start.12 = (bf16[256,2048]{1,0:T(8,128)(2,1)S(1)}, bf16[256,2048]{1,0:T(8,128)(2,1)}, u32[]{:S(2)}) copy-start(bf16[256,2048]{1,0:T(8,128)(2,1)} %copy-done.11) | copy-start | bytes 3145732
Sparse Core Ops, SparseCore 0:
  10.3 110.2 all-gather.1
